TPU v7x, 32 devices: a whole 2x2x4 slice. The times are simulated.
32 devices in a mesh: tm: 8 (over z, y), row: 4 (over x, core).
Axes of the slice: x: 2, y: 2, z: 4, core: 2. Of those that a mesh axis runs over, the one named last changes fastest.
Arguments:
- lower: bfloat16 [16, 1024, 1024], P('tm', 'row'), may hold values from -0.1875 to 0.1875
- upper: bfloat16 [16, 1024, 1024], P('tm', 'row'), may hold values from -0.1875 to 0.1875
- shift_diag: float32 [16, 1024], P('tm', 'row'), may hold values from -0.5 to 0.5
- rhs: float32 [16, 1024, 128], P('tm', 'row'), may hold values from -6 to 6
Outputs:
- lower_two: bfloat16 [16, 1024, 1024], P('tm', 'row')
- upper_two: bfloat16 [16, 1024, 1024], P('tm', 'row')
- excess_two: bfloat16 [16, 1024, 1024], P('tm', 'row')
- rhs_two: float32 [16, 1024, 128], P('tm', 'row')
All inputs are finite; a program needn't handle non-finite values.
Results may differ from a plain program's by a relative error of at most 0.0083.
Values may be sent and summed in bfloat16 or wider, within the bound.
No kernel may reach another device: no remote copies, remote signals or barrier semaphores. Data moves between devices by JAX's collectives and lax.ppermute only.
A program may use at most 128 MiB of HBM per device.

v0:
```python
import jax
import jax.numpy as jnp
from jax import lax
from jax.sharding import PartitionSpec as P


def from_behind(array, axis, by):
    count = lax.axis_size(axis)
    pairs = [(i, i + by) for i in range(count) if 0 <= i + by < count]
    return lax.ppermute(array, axis, pairs)


def stacked(left_blocks, right_blocks):
    return jnp.einsum("bij,bjk->bik", left_blocks, right_blocks, preferred_element_type=jnp.float32)


def neighbour_terms(lower_rows, upper_rows, full_panel, distance):
    below_in = from_behind(full_panel[-distance:], "tm", 1)
    above_in = from_behind(full_panel[:distance], "tm", -1)
    below_panel = jnp.concatenate([below_in, full_panel[:-distance]], axis=0)
    above_panel = jnp.concatenate([full_panel[distance:], above_in], axis=0)
    return (stacked(lower_rows, below_panel), stacked(upper_rows, above_panel))


def apply_terms(below_term, above_term, excess_rows, rhs_rows, states):
    lower_new = (-below_term[:, :, :states]).astype(jnp.bfloat16)
    upper_new = (-above_term[:, :, states : 2 * states]).astype(jnp.bfloat16)
    excess_new = (
        excess_rows - below_term[:, :, states : 2 * states] - above_term[:, :, :states]
    ).astype(jnp.bfloat16)
    rhs_new = rhs_rows - below_term[:, :, 2 * states :] - above_term[:, :, 2 * states :]
    return (lower_new, upper_new, excess_new, rhs_new)


def shards(lower, upper, shift_diag, rhs):
    groups = lower.shape[0]
    height = lower.shape[1]
    states = lower.shape[2]
    offset = lax.axis_index("row") * height
    columns = lax.broadcasted_iota(jnp.int32, (groups, height, states), 2)
    row_pos = lax.broadcasted_iota(jnp.int32, (groups, height, states), 1) + offset
    excess_zero = jnp.where(columns == row_pos, shift_diag[:, :, None], 0.0)
    scaling = 1.0 - shift_diag
    panel_one = (
        scaling[:, :, None]
        * jnp.concatenate([lower.astype(jnp.float32), upper.astype(jnp.float32), rhs], axis=2)
    ).astype(jnp.bfloat16)
    full_one = lax.all_gather(panel_one, "row", axis=1, tiled=True)
    below_one, above_one = neighbour_terms(lower, upper, full_one, 1)
    lower_one, upper_one, excess_one, rhs_one = apply_terms(
        below_one, above_one, excess_zero, rhs, states
    )
    rhs_short = rhs_one.astype(jnp.bfloat16)
    own_rows = jnp.concatenate([lower_one, upper_one, rhs_short], axis=2)
    product = stacked(excess_one, lax.all_gather(own_rows, "row", axis=1, tiled=True))
    panel_two = (own_rows.astype(jnp.float32) - product).astype(jnp.bfloat16)
    full_two = lax.all_gather(panel_two, "row", axis=1, tiled=True)
    below_two, above_two = neighbour_terms(lower_one, upper_one, full_two, 2)
    return apply_terms(below_two, above_two, excess_one.astype(jnp.float32), rhs_one, states)


def solution(mesh):
    return jax.shard_map(
        shards,
        mesh=mesh,
        in_specs=(P("tm", "row", None), P("tm", "row", None), P("tm", "row"), P("tm", "row", None)),
        out_specs=(
            P("tm", "row", None),
            P("tm", "row", None),
            P("tm", "row", None),
            P("tm", "row", None),
        ),
        check_vma=False,
    )
```

profile of v0, /device:TPU:8, one launch (start us, length us, event | category | flops | bytes accessed | tf_op | source)
XLA Modules:
  0.0 850.0 jit_solution(13677663556818642498)
XLA Ops:
  7.2 0.0 all-gather.4.cloned.1.call-start
  7.2 0.7 broadcast_subtract_fusion
  7.9 1.1 copy.10
  9.0 1.5 copy.8
  10.5 0.2 convert_element_type.39
  10.6 1.5 copy.9
  12.1 0.2 convert_element_type.40
  12.3 1.7 fusion.15
  14.0 0.0 all-gather.4.cloned.1.call-update
  14.0 0.0 copy-start.6
  14.0 0.0 all-gather.6.cloned.1.call-start
  14.1 63.7 %all-gather.4.cloned.1.call-done = bf16[2,1024,2176]{1,2,0:T(8,128)(2,1)} async-done(((bf16[2,256,2176]{1,2,0:T(8,128)(2,1)}), bf16[2,1024,2176]{1,2,0:T(8,128)(2,1)}) %all-gather.4.cloned.1.call-update) | async-done | bytes 8912912 | tf_op jit(solution)/shard_map/all_gather | solution.py:48
  77.8 8.2 fusion.24
  86.0 3.4 collective-permute-start
  89.3 3.4 collective-permute-start.1
  92.7 0.0 copy-start.7
  92.7 188.3 %collective-permute-done = bf16[1,1024,2176]{1,2,0:T(8,128)(2,1)} collective-permute-done((bf16[1,1024,2176]{1,2,0:T(8,128)(2,1)}, bf16[1,1024,2176]{1,2,0:T(8,128)(2,1)}, u32[]{:S(2)}, u32[]{:S(2)}) %collective-permute-start) | collective-permute-done | bytes 4456480 | tf_op jit(solution)/shard_map/ppermute | solution.py:10
  281.0 0.0 copy-done.6
  281.0 5.1 fusion.11
  286.1 0.0 copy-start.1
  286.1 0.0 copy-start.8
  286.1 0.0 collective-permute-done.1
  286.1 0.0 copy-done.7
  286.1 6.7 fusion.8
  292.8 0.0 copy-start.2
  292.8 0.1 fusion.23
  292.8 0.0 copy-done.1
  292.9 0.0 copy-done.8
  292.9 0.9 fusion.18
  293.8 1.1 copy-done.2
  294.9 0.0 copy-start.4
  294.9 1.6 pad_maximum_fusion
  296.5 0.0 all-gather.6.cloned.1.call-update
  296.5 0.0 all-gather.8.cloned.1.call-start
  296.6 62.6 %all-gather.6.cloned.1.call-done = bf16[2,1024,2176]{1,2,0:T(8,128)(2,1)} async-done(((bf16[2,256,2176]{1,2,0:T(8,128)(2,1)}), bf16[2,1024,2176]{1,2,0:T(8,128)(2,1)}) %all-gather.6.cloned.1.call-update) | async-done | bytes 8912912 | tf_op jit(solution)/shard_map/all_gather | solution.py:55
  359.2 7.4 fusion.14
  366.6 0.0 copy-done.4
  366.6 0.0 all-gather.8.cloned.1.call-update
  366.6 62.6 %all-gather.8.cloned.1.call-done = bf16[2,1024,2176]{1,2,0:T(8,128)(2,1)} async-done(((bf16[2,256,2176]{1,2,0:T(8,128)(2,1)}), bf16[2,1024,2176]{1,2,0:T(8,128)(2,1)}) %all-gather.8.cloned.1.call-update) | async-done | bytes 8912912 | tf_op jit(solution)/shard_map/all_gather | solution.py:57
  429.2 3.3 collective-permute-start.3
  432.6 2.7 collective-permute-start.2
  435.3 380.9 %collective-permute-done.3 = bf16[2,1024,2176]{1,2,0:T(8,128)(2,1)S(1)} collective-permute-done((bf16[2,1024,2176]{1,2,0:T(8,128)(2,1)}, bf16[2,1024,2176]{1,2,0:T(8,128)(2,1)S(1)}, u32[]{:S(2)}, u32[]{:S(2)}) %collective-permute-start.3) | collective-permute-done | bytes 8912928 | tf_op jit(solution)/shard_map/ppermute | solution.py:10
  816.2 3.2 fusion.28
  819.4 0.0 copy-start.3
  819.4 1.6 fusion.26
  821.0 0.0 collective-permute-done.2
  821.0 5.6 fusion.27
  826.6 0.0 copy-done.3
  826.6 0.7 slice.70
  827.4 0.0 slice-start
  827.4 2.0 fusion.25
  829.4 1.8 copy.33
  831.2 0.0 slice-done
  831.2 0.0 copy-start
  831.2 0.8 copy.35
  832.0 0.0 copy-start.5
  832.0 3.0 copy.32
  835.0 0.0 copy-done
  835.0 0.0 copy-done.5
  835.0 3.0 subtract_convert_fusion
  838.0 2.3 copy.23
  840.3 1.1 copy.34
  841.4 1.2 subtract_subtract_fusion
  842.6 0.8 copy.24
  (1 shorter events, 0.0 us)
Async XLA Ops:
  7.2 70.6 %all-gather.4.cloned.1.call-start = ((), (), s32[]{:S(2)}) async-start(), calls=%async_computation | async-start | bytes 11141120 | tf_op jit(solution)/shard_map/all_gather | solution.py:48
  14.0 267.0 %copy-start.6 = (bf16[2,256,1024]{2,1,0:T(8,128)(2,1)S(1)}, bf16[2,256,1024]{2,1,0:T(8,128)(2,1)}, u32[]{:S(2)}) copy-start(bf16[2,256,1024]{2,1,0:T(8,128)(2,1)} %param.4) | copy-start | bytes 3145732
  14.0 345.2 %all-gather.6.cloned.1.call-start = ((), (), s32[]{:S(2)}) async-start(), calls=%async_computation.1 | async-start | bytes 11141120 | tf_op jit(solution)/shard_map/all_gather | solution.py:55
  86.0 195.0 %collective-permute-start = (bf16[1,1024,2176]{1,2,0:T(8,128)(2,1)}, bf16[1,1024,2176]{1,2,0:T(8,128)(2,1)}, u32[]{:S(2)}, u32[]{:S(2)}) collective-permute-start(bf16[1,1024,2176]{1,2,0:T(8,128)(2,1)} %get-tuple-element.8), channel_id=1, source_target_pairs={{0,4},{4,8},{8,12},{12,16},{16,20},{20,24},{24,28},{1,5},{5,9},{9,... | collective-permute-start | bytes 13369352 | tf_op jit(solution)/shard_map/ppermute | solution.py:10
  89.3 196.8 %collective-permute-start.1 = (bf16[1,1024,2176]{1,2,0:T(8,128)(2,1)}, bf16[1,1024,2176]{1,2,0:T(8,128)(2,1)}, u32[]{:S(2)}, u32[]{:S(2)}) collective-permute-start(bf16[1,1024,2176]{1,2,0:T(8,128)(2,1)} %get-tuple-element.9), channel_id=1, source_target_pairs={{4,0},{8,4},{12,8},{16,12},{20,16},{24,20},{28,24},{5,1},{9,5},{13... | collective-permute-start | bytes 13369352 | tf_op jit(solution)/shard_map/ppermute | solution.py:10
  92.7 193.4 %copy-start.7 = (bf16[2,256,1024]{2,1,0:T(8,128)(2,1)S(1)}, bf16[2,256,1024]{2,1,0:T(8,128)(2,1)}, u32[]{:S(2)}) copy-start(bf16[2,256,1024]{2,1,0:T(8,128)(2,1)} %param.5) | copy-start | bytes 3145732
  286.1 6.8 copy-start.1
  286.1 6.8 copy-start.8
  292.8 2.1 copy-start.2
  294.9 71.7 %copy-start.4 = (bf16[2,256,1024]{1,2,0:T(8,128)(2,1)}, bf16[2,256,1024]{1,2,0:T(8,128)(2,1)S(1)}, u32[]{:S(2)}) copy-start(bf16[2,256,1024]{1,2,0:T(8,128)(2,1)S(1)} %get-tuple-element.14) | copy-start | bytes 3145732
  296.5 132.7 %all-gather.8.cloned.1.call-start = ((), (), s32[]{:S(2)}) async-start(), calls=%async_computation.2 | async-start | bytes 11141120 | tf_op jit(solution)/shard_map/all_gather | solution.py:57
  429.2 386.9 %collective-permute-start.3 = (bf16[2,1024,2176]{1,2,0:T(8,128)(2,1)}, bf16[2,1024,2176]{1,2,0:T(8,128)(2,1)S(1)}, u32[]{:S(2)}, u32[]{:S(2)}) collective-permute-start(bf16[2,1024,2176]{1,2,0:T(8,128)(2,1)} %all-gather.8.cloned.1.call-done), channel_id=1, source_target_pairs={{4,0},{8,4},{12,8},{16,12},{20,16},{24,20},{28,24},{5,1},{9,5},{13... | collective-permute-start | bytes 26738696 | tf_op jit(solution)/shard_map/ppermute | solution.py:10
  432.6 388.4 %collective-permute-start.2 = (bf16[2,1024,2176]{1,2,0:T(8,128)(2,1)}, bf16[2,1024,2176]{1,2,0:T(8,128)(2,1)}, u32[]{:S(2)}, u32[]{:S(2)}) collective-permute-start(bf16[2,1024,2176]{1,2,0:T(8,128)(2,1)} %all-gather.8.cloned.1.call-done), channel_id=1, source_target_pairs={{0,4},{4,8},{8,12},{12,16},{16,20},{20,24},{24,28},{1,5},{5,9},{9,... | collective-permute-start | bytes 26738696 | tf_op jit(solution)/shard_map/ppermute | solution.py:10
  819.4 7.2 copy-start.3
  827.4 3.8 slice-start
  831.2 3.9 copy-start
  832.0 3.0 copy-start.5
Sparse Core Ops, SparseCore 0:
  14.2 63.5 all-gather.3
  296.6 62.5 all-gather.5
  366.7 62.4 all-gather.7
where the time goes:
time: 850 us
  waiting for transfers between devices  758 us (89%)
  matrix products  27.9 us (3%)
  local copies, waits for them, and re-layouts  23.9 us (3%)
  between operations  14 us (2%)
  other arithmetic  13.1 us (2%)
  starting transfers between devices  12.9 us (2%)
    ppermute x4, waiting for transfers between devices, from_behind(): return lax.ppermute(array, axis, pairs)  569 us
    all_gather x1, waiting for transfers between devices, shards(): full_one = lax.all_gather(panel_one, 'row', axis=1, tiled=True)  63.7 us
    all_gather x1, waiting for transfers between devices, shards(): lax.all_gather(own_rows, 'row', axis=1, tiled=True)  62.6 us
    all_gather x1, waiting for transfers between devices, shards(): full_two = lax.all_gather(panel_two, 'row', axis=1, tiled=True)  62.6 us
    dot_general x5, matrix products, stacked(): jnp.einsum('bij,bjk->bik', left_blocks, right_blocks, preferred_element_t...  27.9 us
  transfers between devices with their start and end apart: 7, of which 5 were waited for; matrix products, arithmetic and copies ran while one was open for 1% of the time, Pallas kernels for 0%

commit v1 on v0

v1 whole, which is shorter than its diff:
```python
import jax
import jax.numpy as jnp
from jax import lax
from jax.sharding import PartitionSpec as P

AXES = ("tm", "row")


def from_behind(array, axis, by):
    count = lax.axis_size(axis)
    pairs = [(i, i + by) for i in range(count) if 0 <= i + by < count]
    return lax.ppermute(array, axis, pairs)


def stacked(left_blocks, right_blocks):
    return jnp.einsum("bij,bjk->bik", left_blocks, right_blocks, preferred_element_type=jnp.float32)


def neighbour_terms(lower_rows, upper_rows, panel_rows, distance):
    below_in = from_behind(panel_rows[-distance:], "tm", 1)
    above_in = from_behind(panel_rows[:distance], "tm", -1)
    below_panel = jnp.concatenate([below_in, panel_rows[:-distance]], axis=0)
    above_panel = jnp.concatenate([panel_rows[distance:], above_in], axis=0)
    below_full = lax.all_gather(below_panel, "row", axis=1, tiled=True)
    above_full = lax.all_gather(above_panel, "row", axis=1, tiled=True)
    return (stacked(lower_rows, below_full), stacked(upper_rows, above_full))


def apply_terms(below_term, above_term, excess_rows, rhs_rows, states):
    lower_new = (-below_term[:, :, :states]).astype(jnp.bfloat16)
    upper_new = (-above_term[:, :, states : 2 * states]).astype(jnp.bfloat16)
    excess_new = (
        excess_rows - below_term[:, :, states : 2 * states] - above_term[:, :, :states]
    ).astype(jnp.bfloat16)
    rhs_new = rhs_rows - below_term[:, :, 2 * states :] - above_term[:, :, 2 * states :]
    return (lower_new, upper_new, excess_new, rhs_new)


def shards_by_rows(lower, upper, shift_diag, rhs):
    groups, height, states = lower.shape
    offset = lax.axis_index("row") * height
    columns = lax.broadcasted_iota(jnp.int32, (groups, height, states), 2)
    row_pos = lax.broadcasted_iota(jnp.int32, (groups, height, states), 1) + offset
    excess_zero = jnp.where(columns == row_pos, shift_diag[:, :, None], 0.0)
    panel_one = scaled_panel(lower, upper, shift_diag, rhs)
    below_one, above_one = neighbour_terms(lower, upper, panel_one, 1)
    lower_one, upper_one, excess_one, rhs_one = apply_terms(
        below_one, above_one, excess_zero, rhs, states
    )
    own_rows = jnp.concatenate([lower_one, upper_one, rhs_one.astype(jnp.bfloat16)], axis=2)
    product = stacked(excess_one, lax.all_gather(own_rows, "row", axis=1, tiled=True))
    panel_two = (own_rows.astype(jnp.float32) - product).astype(jnp.bfloat16)
    below_two, above_two = neighbour_terms(lower_one, upper_one, panel_two, 2)
    return apply_terms(below_two, above_two, excess_one.astype(jnp.float32), rhs_one, states)


def scaled_panel(lower, upper, shift_diag, rhs):
    scaling = (1.0 - shift_diag)[..., None]
    parts = [lower.astype(jnp.float32), upper.astype(jnp.float32), rhs]
    return (scaling * jnp.concatenate(parts, axis=-1)).astype(jnp.bfloat16)


def dot(left, right):
    return jnp.dot(left, right, preferred_element_type=jnp.float32)


def shards_by_blocks(lower, upper, shift_diag, rhs):
    height, states = lower.shape[1:]
    scenarios = rhs.shape[2]
    half = states // 2
    planes = lax.axis_size("tm") // 2
    group, row = lax.axis_index("tm"), lax.axis_index("row")
    y, z, x, k = group % 2, group // 2, row // 2, row % 2
    home = k == y

    def send(array, to):
        pairs = []
        for device in range(planes * 8):
            gz, gy, gx, gk = device // 8, device // 4 % 2, device // 2 % 2, device % 2
            target = to(gx, gy, gz, gk)
            if target is not None and 0 <= target[2] < planes:
                tx, ty, tz, tk = target
                pairs.append((device, tz * 8 + ty * 4 + tx * 2 + tk))
        return lax.ppermute(array, AXES, pairs)

    def swap(array):
        return send(array, lambda x, y, z, k: (x, y, z, 1 - k))

    def across_x(array):
        return send(array, lambda x, y, z, k: (1 - x, y, z, k))

    def to_away(array):
        first = send(array, lambda x, y, z, k: (x, 1 - y, z, y) if k == y else None)
        second = send(array, lambda x, y, z, k: (x, 1 - y, z, y) if k != y else None)
        return first, second

    def away_x(array):
        return send(array, lambda x, y, z, k: (1 - x, y, z, k) if k != y else None)

    def away_to_home_z(array):
        return send(array, lambda x, y, z, k: (x, y, z + 1 - 2 * y, y) if k != y else None)

    quarters = scaled_panel(lower, upper, shift_diag, rhs)
    outer = lax.dynamic_index_in_dim(quarters, y, 0, False)
    inner = lax.dynamic_index_in_dim(quarters, 1 - y, 0, False)
    shifts = lax.all_gather(shift_diag, AXES, axis=0, tiled=False)

    far_a, far_b = to_away(outer)
    inner_x = across_x(inner)
    inner_k = swap(inner)
    outer_k = send(outer, lambda x, y, z, k: (x, y, z, y) if k != y else None)
    centre_a, centre_b = to_away(inner)
    far_xa, far_xb = away_x(far_a), away_x(far_b)
    halo_a, halo_b = away_to_home_z(far_b), away_to_home_z(far_a)
    outer_late, _ = lax.optimization_barrier((outer, (far_a, far_b)))
    outer_xa = send(outer_late, lambda x, y, z, k: (1 - x, y, z, y) if k == y else None)
    outer_xb = send(outer_late, lambda x, y, z, k: (1 - x, y, z, y) if k != y else None)
    inner_xk = swap(inner_x)
    centre_xa, centre_xb = to_away(inner_x)
    halo_xa, halo_xb = away_to_home_z(far_xb), away_to_home_z(far_xa)

    def assembled(own_a, own_b, other_a, other_b):
        panel = jnp.zeros((states, 2 * states + scenarios), jnp.bfloat16)
        for piece, px, pk in (
            (own_a, x, k), (own_b, x, 1 - k), (other_a, 1 - x, k), (other_b, 1 - x, 1 - k)
        ):
            panel = lax.dynamic_update_slice_in_dim(panel, piece, px * half + pk * height, 0)
        return panel

    def pick(at_home, away):
        return jnp.where(home, at_home, away)

    near = assembled(inner, inner_k, inner_x, inner_xk)
    far = assembled(
        pick(halo_a, far_a), pick(halo_b, far_b), pick(halo_xa, far_xa), pick(halo_xb, far_xb)
    )
    centre = assembled(
        pick(outer, centre_a), pick(outer_k, centre_b),
        pick(outer_xa, centre_xa), pick(outer_xb, centre_xb),
    )

    near_at, far_at = (1 - k) * states, k * states

    def columns(array, at, width=states):
        return lax.dynamic_slice_in_dim(array, at, width, 1)

    shift = lax.dynamic_slice_in_dim(shifts, (2 * z + k) * 4, 4, 0)
    shift = lax.dynamic_index_in_dim(shift, y, 1, False).reshape(states, 1)
    unscale = 1.0 / (1.0 - shift)
    near_term = unscale * dot(columns(centre, near_at), near)
    far_term = unscale * dot(columns(centre, far_at), far)
    near_one = (-columns(near_term, near_at)).astype(jnp.bfloat16)
    far_one = (-columns(far_term, far_at)).astype(jnp.bfloat16)
    diagonal = jnp.where(
        lax.broadcasted_iota(jnp.int32, (states, states), 0)
        == lax.broadcasted_iota(jnp.int32, (states, states), 1),
        shift, 0.0,
    )
    excess_one = (diagonal - columns(near_term, far_at) - columns(far_term, near_at)).astype(
        jnp.bfloat16
    )
    rhs_one = (
        unscale * centre[:, 2 * states :].astype(jnp.float32)
        - near_term[:, 2 * states :]
        - far_term[:, 2 * states :]
    )

    own = jnp.concatenate(
        [columns(near_one, x * half, half), columns(far_one, x * half, half),
         rhs_one.astype(jnp.bfloat16)], axis=1,
    )
    panel_two = (own.astype(jnp.float32) - dot(excess_one, own)).astype(jnp.bfloat16)
    near_two = swap(panel_two)
    far_two = send(panel_two, lambda x, y, z, k: (x, y, z - 1 + 2 * k, 1 - k))
    near_out = dot(near_one, near_two)
    far_out = dot(far_one, far_two)
    near_new = (-near_out[:, half:states]).astype(jnp.bfloat16)
    far_new = (-far_out[:, :half]).astype(jnp.bfloat16)
    excess_new = (
        columns(excess_one, x * half, half).astype(jnp.float32)
        - near_out[:, :half]
        - far_out[:, half:states]
    ).astype(jnp.bfloat16)
    rhs_new = rhs_one - near_out[:, states:] - far_out[:, states:]

    def at_home(array, width, crosses=(0, 1)):
        placed = jnp.zeros((2, height, width), array.dtype)
        for other_x in crosses:
            for flip in (0, 1):
                at = (x ^ other_x) * half + (y ^ flip) * height
                piece = lax.dynamic_slice_in_dim(array, at, height, 0)
                piece = send(piece, lambda x, y, z, k: (x ^ other_x, k, z, y ^ flip))
                start = (k ^ flip, 0, (x ^ other_x) * half if len(crosses) > 1 else 0)
                placed = lax.dynamic_update_slice(placed, piece[None], start)
        return placed

    near_home, far_home, excess_home = (
        at_home(part, states) for part in (near_new, far_new, excess_new)
    )
    rhs_home = at_home(rhs_new, scenarios, (0,))
    lower_two = jnp.where(y == 0, far_home, near_home)
    upper_two = jnp.where(y == 0, near_home, far_home)
    return lower_two, upper_two, excess_home, rhs_home


def solution(mesh):
    paired = mesh.shape["row"] == 4 and mesh.shape["tm"] % 2 == 0
    spec = P("tm", "row", None)

    def program(lower, upper, shift_diag, rhs):
        two_blocks = lower.shape[0] == 2 * mesh.shape["tm"]
        return jax.shard_map(
            shards_by_blocks if paired and two_blocks else shards_by_rows,
            mesh=mesh,
            in_specs=(spec, spec, P("tm", "row"), spec),
            out_specs=(spec,) * 4,
            check_vma=False,
        )(lower, upper, shift_diag, rhs)

    return program
```

time: 850 us -> 279 us (0.33)
  waiting for transfers between devices: 758 us -> 133 us
  blocking collectives: 0 us -> 37.9 us
  starting transfers between devices: 12.9 us -> 44.6 us
  between operations: 14 us -> 1.48 us
  local copies, waits for them, and re-layouts: 23.9 us -> 13.8 us
    ppermute x4 -> x34, waiting for transfers between devices: 569 us -> 133 us  [send(): return lax.ppermute(array, AXES, pairs)]
    all_gather x3 -> x0, waiting for transfers between devices: 189 us -> none  [the longest x1 63.7 us: shards(): full_one = lax.all_gather(panel_one, 'row', axis=1, tiled=True)]
    all_gather x0 -> x1, blocking collectives: none -> 37.9 us  [shards_by_blocks(): shifts = lax.all_gather(shift_diag, AXES, axis=0, tiled=False)]
    ppermute x4 -> x34, starting transfers between devices: 12.7 us -> 44.6 us  [send(): return lax.ppermute(array, AXES, pairs)]
    unnamed x27 -> x20, local copies, waits for them, and re-layouts: 15 us -> 2.38 us
    slice x4 -> x0, local copies, waits for them, and re-layouts: 8.88 us -> none  [the longest x1 8.16 us: neighbour_terms(): below_in = from_behind(full_panel[-distance:], 'tm', 1)]
  transfers between devices with their start and end apart: 7 -> 34, of which waited for: 5 -> 14; matrix products, arithmetic and copies ran while one was open for 1% -> 9% of each run, Pallas kernels for 0% -> 0%
where the time goes in v1:
time: 279 us; the launch traced here: 277 us
  waiting for transfers between devices  133 us (48%)
  starting transfers between devices  44.6 us (16%)
  blocking collectives  37.9 us (14%)
  matrix products  29 us (10%)
  other arithmetic  17.3 us (6%)
  local copies, waits for them, and re-layouts  13.8 us (5%)
    ppermute x34, waiting for transfers between devices, send(): return lax.ppermute(array, AXES, pairs)  133 us
    ppermute x34, starting transfers between devices, send(): return lax.ppermute(array, AXES, pairs)  44.6 us
    all_gather x1, blocking collectives, shards_by_blocks(): shifts = lax.all_gather(shift_diag, AXES, axis=0, tiled=False)  37.9 us
    dot_general x5, matrix products, dot(): return jnp.dot(left, right, preferred_element_type=jnp.float32)  29 us
    dynamic_update_slice x4, local copies, waits for them, and re-layouts, assembled(): lax.dynamic_update_slice_in_dim(panel, piece, px * half + pk * height, 0)  7.26 us
    convert_element_type x2, other arithmetic, scaled_panel(): parts = [lower.astype(jnp.float32), upper.astype(jnp.float32), rhs]  5.65 us
  transfers between devices with their start and end apart: 34, of which 14 were waited for; matrix products, arithmetic and copies ran while one was open for 9% of the time, Pallas kernels for 0%

profile of v1, /device:TPU:8, one launch (start us, length us, event | category | flops | bytes accessed | tf_op | source)
XLA Modules:
  0.0 276.8 jit_solution(17939942524355345140)
XLA Ops:
  0.7 2.9 %convert_element_type.42 = f32[2,256,1024]{2,1,0:T(8,128)} convert(bf16[2,256,1024]{2,1,0:T(8,128)(2,1)} %param.4) | non-fusion elementwise | flops 524288 | bytes 3145728 | tf_op jit(solution)/shard_map/convert_element_type | solution.py:59
  3.5 2.8 %convert_element_type.43 = f32[2,256,1024]{2,1,0:T(8,128)} convert(bf16[2,256,1024]{2,1,0:T(8,128)(2,1)} %param.5) | non-fusion elementwise | flops 524288 | bytes 3145728 | tf_op jit(solution)/shard_map/convert_element_type | solution.py:59
  6.4 2.5 fusion
  8.9 2.4 broadcast.26.clone
  11.3 1.5 constant_dynamic-update-slice_fusion.3
  12.8 4.5 %collective-permute-start = (bf16[256,2176]{1,0:T(8,128)(2,1)}, bf16[256,2176]{1,0:T(8,128)(2,1)}, u32[]{:S(2)}, u32[]{:S(2)}) collective-permute-start(bf16[256,2176]{1,0:T(8,128)(2,1)} %get-tuple-element.7), channel_id=1, source_target_pairs={{0,4},{2,6},{5,1},{7,3},{8,12},{10,14},{13,9},{15,11},{16,20},{18,... | collective-permute-start | bytes 3342344 | tf_op jit(solution)/shard_map/ppermute | solution.py:84
  17.3 1.5 collective-permute-start.6
  18.8 0.7 collective-permute-start.2
  19.7 19.4 %collective-permute-done = bf16[256,2176]{1,0:T(8,128)(2,1)} collective-permute-done((bf16[256,2176]{1,0:T(8,128)(2,1)}, bf16[256,2176]{1,0:T(8,128)(2,1)}, u32[]{:S(2)}, u32[]{:S(2)}) %collective-permute-start) | collective-permute-done | bytes 1114144 | tf_op jit(solution)/shard_map/ppermute | solution.py:84
  39.4 0.4 select_dynamic-update-slice_fusion.7
  39.8 0.7 collective-permute-start.4
  40.5 6.9 %collective-permute-start.3 = (bf16[256,2176]{1,0:T(8,128)(2,1)S(1)}, bf16[256,2176]{1,0:T(8,128)(2,1)S(1)}, u32[]{:S(2)}, u32[]{:S(2)}) collective-permute-start(bf16[256,2176]{1,0:T(8,128)(2,1)S(1)} %get-tuple-element.5), channel_id=1, source_target_pairs={{0,4},{2,6},{5,1},{7,3},{8,12},{10,14},{13,9},{15,11},{16,20},{18,... | collective-permute-start | bytes 3342344 | tf_op jit(solution)/shard_map/ppermute | solution.py:84
  47.4 1.3 collective-permute-start.1
  48.7 37.9 %all-gather.1 = f32[32,2,256]{2,1,0:T(2,128)S(1)} all-gather(f32[1,2,256]{2,1,0:T(2,128)S(1)} %bitcast.45), channel_id=2, replica_groups=mesh['tm'=8,'row'=4] {'tm','row'}, dimensions={0}, use_global_device_ids=true | all-gather | bytes 67584 | tf_op jit(solution)/shard_map/all_gather | solution.py:106
  86.6 0.4 collective-permute-start.17
  87.0 2.3 constant_dynamic-update-slice_fusion.2
  89.4 2.3 constant_dynamic-update-slice_fusion.1
  91.7 1.3 collective-permute-start.7
  93.1 0.7 collective-permute-start.9
  93.8 1.9 collective-permute-start.5
  95.8 1.3 collective-permute-start.8
  97.4 1.3 collective-permute-start.10
  98.7 1.1 constant_dynamic-update-slice_fusion
  99.8 17.0 %collective-permute-done.7 = bf16[256,2176]{1,0:T(8,128)(2,1)S(1)} collective-permute-done((bf16[256,2176]{1,0:T(8,128)(2,1)}, bf16[256,2176]{1,0:T(8,128)(2,1)S(1)}, u32[]{:S(2)}, u32[]{:S(2)}) %collective-permute-start.7) | collective-permute-done | bytes 1114144 | tf_op jit(solution)/shard_map/ppermute | solution.py:84
  116.8 1.3 collective-permute-start.11
  118.0 3.7 %collective-permute-done.5 = bf16[256,2176]{1,0:T(8,128)(2,1)S(1)} collective-permute-done((bf16[256,2176]{1,0:T(8,128)(2,1)S(1)}, bf16[256,2176]{1,0:T(8,128)(2,1)S(1)}, u32[]{:S(2)}, u32[]{:S(2)}) %collective-permute-start.5) | collective-permute-done | bytes 1114144 | tf_op jit(solution)/shard_map/ppermute | solution.py:84
  121.7 0.7 collective-permute-start.12
  122.8 0.7 collective-permute-start.14
  123.6 0.4 select_dynamic-update-slice_fusion.4
  124.0 8.9 %convolution_multiply_fusion = f32[1024,2176]{1,0:T(8,128)S(1)} fusion(bf16[1024,2176]{1,0:T(8,128)(2,1)} %constant_dynamic-update-slice_fusion, f32[1024]{0:T(1024)S(1)} %subtract_divide_fusion, bf16[1024,2176]{1,0:T(8,128)(2,1)S(1)} %select_dynamic-update-slice_fusion.4, s32[]{:T(128)S(6)} %select_n.199), kind=kOutput, calls=%fused_computation | convolution fusion | flops 4565630976 | bytes 15470596 | tf_op jit(solution)/shard_map/dot_general | solution.py:64
  133.0 1.3 collective-permute-start.13
  134.3 1.5 collective-permute-start.15
  136.1 0.4 select_dynamic-update-slice_fusion.3
  136.4 3.1 %collective-permute-done.11 = bf16[256,2176]{1,0:T(8,128)(2,1)S(1)} collective-permute-done((bf16[256,2176]{1,0:T(8,128)(2,1)S(1)}, bf16[256,2176]{1,0:T(8,128)(2,1)S(1)}, u32[]{:S(2)}, u32[]{:S(2)}) %collective-permute-start.11) | collective-permute-done | bytes 1114144 | tf_op jit(solution)/shard_map/ppermute | solution.py:84
  139.9 17.3 %collective-permute-done.13 = bf16[256,2176]{1,0:T(8,128)(2,1)S(1)} collective-permute-done((bf16[256,2176]{1,0:T(8,128)(2,1)S(1)}, bf16[256,2176]{1,0:T(8,128)(2,1)S(1)}, u32[]{:S(2)}, u32[]{:S(2)}) %collective-permute-start.13) | collective-permute-done | bytes 1114144 | tf_op jit(solution)/shard_map/ppermute | solution.py:84
  157.5 11.6 %collective-permute-done.15 = bf16[256,2176]{1,0:T(8,128)(2,1)S(1)} collective-permute-done((bf16[256,2176]{1,0:T(8,128)(2,1)S(1)}, bf16[256,2176]{1,0:T(8,128)(2,1)S(1)}, u32[]{:S(2)}, u32[]{:S(2)}) %collective-permute-start.15) | collective-permute-done | bytes 1114144 | tf_op jit(solution)/shard_map/ppermute | solution.py:84
  169.4 5.0 %convolution_multiply_fusion.1 = f32[1024,2176]{1,0:T(8,128)S(1)} fusion(bf16[1024,2176]{1,0:T(8,128)(2,1)S(1)} %select_dynamic-update-slice_fusion, f32[1024]{0:T(1024)S(1)} %subtract_divide_fusion, bf16[1024,2176]{1,0:T(8,128)(2,1)S(1)} %select_dynamic-update-slice_fusion.4, s32[]{:T(128)S(6)} %select_n.194), kind=kOutput, calls=%fused_computation.1 | convolution fusion | flops 4565630976 | bytes 15470596 | tf_op jit(solution)/shard_map/dot_general | solution.py:64
  174.5 2.1 negate_convert_fusion
  176.6 1.4 copy-done.1
  178.5 5.3 %subtract_convert_fusion = bf16[1024,1152]{1,0:T(8,128)(2,1)} fusion(bf16[1024,1024]{1,0:T(8,128)(2,1)S(1)} %get-tuple-element.11, bf16[1024,128]{1,0:T(8,128)(2,1)S(1)} %fusion.14, bf16[1024,512]{1,0:T(8,128)(2,1)S(1)} %get-tuple-element.32, bf16[1024,512]{1,0:T(8,128)(2,1)S(1)} %get-tuple-element.33), kind=kOutput, calls=%fused_computation.2 | convolution fusion | flops 2432434176 | bytes 6815744 | tf_op jit(solution)/shard_map/dot_general | solution.py:64
  183.8 2.1 collective-permute-start.18
  186.0 2.7 collective-permute-done.23
  188.7 5.2 %fusion.16 = f32[1024,1152]{1,0:T(8,128)S(1)} fusion(bf16[1024,1024]{1,0:T(8,128)(2,1)} %copy-done.5, bf16[1024,1152]{1,0:T(8,128)(2,1)} %collective-permute-done.23), kind=kOutput, calls=%fused_computation.81 | convolution fusion | flops 2415919104 | bytes 9175040 | tf_op jit(solution)/shard_map/dot_general | solution.py:64
  193.9 20.4 %collective-permute-done.18 = bf16[1024,1152]{1,0:T(8,128)(2,1)} collective-permute-done((bf16[1024,1152]{1,0:T(8,128)(2,1)}, bf16[1024,1152]{1,0:T(8,128)(2,1)}, u32[]{:S(2)}, u32[]{:S(2)}) %collective-permute-start.18) | collective-permute-done | bytes 2359328 | tf_op jit(solution)/shard_map/ppermute | solution.py:84
  214.3 4.5 %fusion.15 = f32[1024,1152]{1,0:T(8,128)S(1)} fusion(bf16[1024,1024]{1,0:T(8,128)(2,1)S(1)} %copy-done.4, bf16[1024,1152]{1,0:T(8,128)(2,1)} %collective-permute-done.18), kind=kOutput, calls=%fused_computation.80 | convolution fusion | flops 2415919104 | bytes 9175040 | tf_op jit(solution)/shard_map/dot_general | solution.py:64
  218.9 1.5 slice_subtract_fusion.2
  220.4 0.9 fusion.6
  221.4 0.7 collective-permute-start.32
  222.0 2.8 %collective-permute-start.33 = (f32[256,128]{1,0:T(8,128)S(1)}, f32[256,128]{1,0:T(8,128)S(1)}, u32[]{:S(2)}, u32[]{:S(2)}) collective-permute-start(f32[256,128]{1,0:T(8,128)S(1)} %get-tuple-element.30), channel_id=1, source_target_pairs={{0,1},{1,5},{2,3},{3,7},{4,0},{5,4},{6,2},{7,6},{8,9},{9,13},{10,1... | collective-permute-start | bytes 393224 | tf_op jit(solution)/shard_map/ppermute | solution.py:84
  224.9 0.7 collective-permute-start.28
  225.6 2.0 collective-permute-start.29
  228.1 0.7 collective-permute-start.19
  228.8 0.9 collective-permute-done.33
  229.7 1.6 collective-permute-start.20
  231.4 1.8 collective-permute-start.21
  233.3 10.8 %collective-permute-done.20 = bf16[256,512]{1,0:T(8,128)(2,1)S(1)} collective-permute-done((bf16[256,512]{1,0:T(8,128)(2,1)S(1)}, bf16[256,512]{1,0:T(8,128)(2,1)S(1)}, u32[]{:S(2)}, u32[]{:S(2)}) %collective-permute-start.20) | collective-permute-done | bytes 262176 | tf_op jit(solution)/shard_map/ppermute | solution.py:84
  244.1 0.7 collective-permute-start.24
  244.8 8.7 %collective-permute-done.22 = bf16[256,512]{1,0:T(8,128)(2,1)S(1)} collective-permute-done((bf16[256,512]{1,0:T(8,128)(2,1)S(1)}, bf16[256,512]{1,0:T(8,128)(2,1)S(1)}, u32[]{:S(2)}, u32[]{:S(2)}) %collective-permute-start.22) | collective-permute-done | bytes 262176 | tf_op jit(solution)/shard_map/ppermute | solution.py:84
  253.9 6.5 %collective-permute-done.25 = bf16[256,512]{1,0:T(8,128)(2,1)S(1)} collective-permute-done((bf16[256,512]{1,0:T(8,128)(2,1)S(1)}, bf16[256,512]{1,0:T(8,128)(2,1)S(1)}, u32[]{:S(2)}, u32[]{:S(2)}) %collective-permute-start.25) | collective-permute-done | bytes 262176 | tf_op jit(solution)/shard_map/ppermute | solution.py:84
  260.4 3.0 %collective-permute-start.31 = (bf16[256,512]{1,0:T(8,128)(2,1)S(1)}, bf16[256,512]{1,0:T(8,128)(2,1)S(1)}, u32[]{:S(2)}, u32[]{:S(2)}) collective-permute-start(bf16[256,512]{1,0:T(8,128)(2,1)S(1)} %get-tuple-element.18), channel_id=1, source_target_pairs={{0,3},{1,7},{2,1},{3,5},{4,2},{5,6},{6,0},{7,4},{8,11},{9,15},{10,... | collective-permute-start | bytes 786440 | tf_op jit(solution)/shard_map/ppermute | solution.py:84
  263.4 8.9 %collective-permute-done.27 = bf16[256,512]{1,0:T(8,128)(2,1)S(1)} collective-permute-done((bf16[256,512]{1,0:T(8,128)(2,1)S(1)}, bf16[256,512]{1,0:T(8,128)(2,1)S(1)}, u32[]{:S(2)}, u32[]{:S(2)}) %collective-permute-start.27) | collective-permute-done | bytes 262176 | tf_op jit(solution)/shard_map/ppermute | solution.py:84
  272.3 1.5 broadcast_select_fusion
  274.0 1.8 collective-permute-done.31
  275.8 1.0 copy-done.6
  (79 shorter events, 4.4 us)
Async XLA Ops:
  0.6 5.7 %copy-start.9 = (f32[2,256]{1,0:T(2,128)S(1)}, f32[2,256]{1,0:T(2,128)}, u32[]{:S(2)}) copy-start(f32[2,256]{1,0:T(2,128)} %param.6) | copy-start | bytes 6148
  0.6 5.7 %copy-start.7 = (f32[2,256,128]{2,1,0:T(8,128)S(1)}, f32[2,256,128]{2,1,0:T(8,128)}, u32[]{:S(2)}) copy-start(f32[2,256,128]{2,1,0:T(8,128)} %param.7) | copy-start | bytes 786436
  12.8 26.3 %collective-permute-start = (bf16[256,2176]{1,0:T(8,128)(2,1)}, bf16[256,2176]{1,0:T(8,128)(2,1)}, u32[]{:S(2)}, u32[]{:S(2)}) collective-permute-start(bf16[256,2176]{1,0:T(8,128)(2,1)} %get-tuple-element.7), channel_id=1, source_target_pairs={{0,4},{2,6},{5,1},{7,3},{8,12},{10,14},{13,9},{15,11},{16,20},{18,... | collective-permute-start | bytes 3342344 | tf_op jit(solution)/shard_map/ppermute | solution.py:84
  17.3 30.2 %collective-permute-start.6 = (bf16[256,2176]{1,0:T(8,128)(2,1)}, bf16[256,2176]{1,0:T(8,128)(2,1)}, u32[]{:S(2)}, u32[]{:S(2)}) collective-permute-start(bf16[256,2176]{1,0:T(8,128)(2,1)} %get-tuple-element.7), channel_id=1, source_target_pairs={{0,2},{1,3},{2,0},{3,1},{4,6},{5,7},{6,4},{7,5},{8,10},{9,11},{10,... | collective-permute-start | bytes 3342344 | tf_op jit(solution)/shard_map/ppermute | solution.py:84
  18.8 75.0 %collective-permute-start.2 = (bf16[256,2176]{1,0:T(8,128)(2,1)}, bf16[256,2176]{1,0:T(8,128)(2,1)S(1)}, u32[]{:S(2)}, u32[]{:S(2)}) collective-permute-start(bf16[256,2176]{1,0:T(8,128)(2,1)} %get-tuple-element.7), channel_id=1, source_target_pairs={{1,4},{3,6},{4,1},{6,3},{9,12},{11,14},{12,9},{14,11},{17,20},{19,... | collective-permute-start | bytes 3342344 | tf_op jit(solution)/shard_map/ppermute | solution.py:84
  19.5 67.1 %collective-permute-start.16 = (bf16[256,2176]{1,0:T(8,128)(2,1)}, bf16[256,2176]{1,0:T(8,128)(2,1)}, u32[]{:S(2)}, u32[]{:S(2)}) collective-permute-start(bf16[256,2176]{1,0:T(8,128)(2,1)} %get-tuple-element.7), channel_id=1, source_target_pairs={{0,1},{1,0},{2,3},{3,2},{4,5},{5,4},{6,7},{7,6},{8,9},{9,8},{10,11... | collective-permute-start | bytes 3342344 | tf_op jit(solution)/shard_map/ppermute | solution.py:84
  39.8 51.9 %collective-permute-start.4 = (bf16[256,2176]{1,0:T(8,128)(2,1)S(1)}, bf16[256,2176]{1,0:T(8,128)(2,1)S(1)}, u32[]{:S(2)}, u32[]{:S(2)}) collective-permute-start(bf16[256,2176]{1,0:T(8,128)(2,1)S(1)} %get-tuple-element.5), channel_id=1, source_target_pairs={{1,4},{3,6},{4,1},{6,3},{9,12},{11,14},{12,9},{14,11},{17,20},{19,... | collective-permute-start | bytes 3342344 | tf_op jit(solution)/shard_map/ppermute | solution.py:84
  40.5 52.5 %collective-permute-start.3 = (bf16[256,2176]{1,0:T(8,128)(2,1)S(1)}, bf16[256,2176]{1,0:T(8,128)(2,1)S(1)}, u32[]{:S(2)}, u32[]{:S(2)}) collective-permute-start(bf16[256,2176]{1,0:T(8,128)(2,1)S(1)} %get-tuple-element.5), channel_id=1, source_target_pairs={{0,4},{2,6},{5,1},{7,3},{8,12},{10,14},{13,9},{15,11},{16,20},{18,... | collective-permute-start | bytes 3342344 | tf_op jit(solution)/shard_map/ppermute | solution.py:84
  47.4 48.3 %collective-permute-start.1 = (bf16[256,2176]{1,0:T(8,128)(2,1)S(1)}, bf16[256,2176]{1,0:T(8,128)(2,1)S(1)}, u32[]{:S(2)}, u32[]{:S(2)}) collective-permute-start(bf16[256,2176]{1,0:T(8,128)(2,1)S(1)} %get-tuple-element.5), channel_id=1, source_target_pairs={{1,0},{3,2},{4,5},{6,7},{9,8},{11,10},{12,13},{14,15},{17,16},{19,... | collective-permute-start | bytes 3342344 | tf_op jit(solution)/shard_map/ppermute | solution.py:84
  86.6 10.8 %collective-permute-start.17 = (bf16[256,2176]{1,0:T(8,128)(2,1)}, bf16[256,2176]{1,0:T(8,128)(2,1)S(1)}, u32[]{:S(2)}, u32[]{:S(2)}) collective-permute-start(bf16[256,2176]{1,0:T(8,128)(2,1)} %collective-permute-done.6), channel_id=1, source_target_pairs={{0,1},{1,0},{2,3},{3,2},{4,5},{5,4},{6,7},{7,6},{8,9},{9,8},{10,11... | collective-permute-start | bytes 3342344 | tf_op jit(solution)/shard_map/ppermute | solution.py:84
  91.7 25.0 %collective-permute-start.7 = (bf16[256,2176]{1,0:T(8,128)(2,1)}, bf16[256,2176]{1,0:T(8,128)(2,1)S(1)}, u32[]{:S(2)}, u32[]{:S(2)}) collective-permute-start(bf16[256,2176]{1,0:T(8,128)(2,1)} %collective-permute-done.6), channel_id=1, source_target_pairs={{0,4},{2,6},{5,1},{7,3},{8,12},{10,14},{13,9},{15,11},{16,20},{18,... | collective-permute-start | bytes 3342344 | tf_op jit(solution)/shard_map/ppermute | solution.py:84
  93.1 29.7 %collective-permute-start.9 = (bf16[256,2176]{1,0:T(8,128)(2,1)}, bf16[256,2176]{1,0:T(8,128)(2,1)S(1)}, u32[]{:S(2)}, u32[]{:S(2)}) collective-permute-start(bf16[256,2176]{1,0:T(8,128)(2,1)} %collective-permute-done.6), channel_id=1, source_target_pairs={{1,4},{3,6},{4,1},{6,3},{9,12},{11,14},{12,9},{14,11},{17,20},{19,... | collective-permute-start | bytes 3342344 | tf_op jit(solution)/shard_map/ppermute | solution.py:84
  93.8 27.9 %collective-permute-start.5 = (bf16[256,2176]{1,0:T(8,128)(2,1)S(1)}, bf16[256,2176]{1,0:T(8,128)(2,1)S(1)}, u32[]{:S(2)}, u32[]{:S(2)}) collective-permute-start(bf16[256,2176]{1,0:T(8,128)(2,1)S(1)} %get-tuple-element.5), channel_id=1, source_target_pairs={{0,2},{2,0},{5,7},{7,5},{8,10},{10,8},{13,15},{15,13},{16,18},{18,... | collective-permute-start | bytes 3342344 | tf_op jit(solution)/shard_map/ppermute | solution.py:84
  95.8 27.8 %collective-permute-start.8 = (bf16[256,2176]{1,0:T(8,128)(2,1)S(1)}, bf16[256,2176]{1,0:T(8,128)(2,1)S(1)}, u32[]{:S(2)}, u32[]{:S(2)}) collective-permute-start(bf16[256,2176]{1,0:T(8,128)(2,1)S(1)} %get-tuple-element.5), channel_id=1, source_target_pairs={{1,2},{3,0},{4,7},{6,5},{9,10},{11,8},{12,15},{14,13},{17,18},{19,... | collective-permute-start | bytes 3342344 | tf_op jit(solution)/shard_map/ppermute | solution.py:84
  97.4 38.3 %collective-permute-start.10 = (bf16[256,2176]{1,0:T(8,128)(2,1)S(1)}, bf16[256,2176]{1,0:T(8,128)(2,1)S(1)}, u32[]{:S(2)}, u32[]{:S(2)}) collective-permute-start(bf16[256,2176]{1,0:T(8,128)(2,1)S(1)} %collective-permute-done.4), channel_id=1, source_target_pairs={{1,8},{3,10},{9,16},{11,18},{12,5},{14,7},{17,24},{19,26},{20,13},... | collective-permute-start | bytes 3342344 | tf_op jit(solution)/shard_map/ppermute | solution.py:84
  116.8 22.8 %collective-permute-start.11 = (bf16[256,2176]{1,0:T(8,128)(2,1)S(1)}, bf16[256,2176]{1,0:T(8,128)(2,1)S(1)}, u32[]{:S(2)}, u32[]{:S(2)}) collective-permute-start(bf16[256,2176]{1,0:T(8,128)(2,1)S(1)} %collective-permute-done.3), channel_id=1, source_target_pairs={{1,8},{3,10},{9,16},{11,18},{12,5},{14,7},{17,24},{19,26},{20,13},... | collective-permute-start | bytes 3342344 | tf_op jit(solution)/shard_map/ppermute | solution.py:84
  121.7 11.2 %collective-permute-start.12 = (bf16[256,2176]{1,0:T(8,128)(2,1)S(1)}, bf16[256,2176]{1,0:T(8,128)(2,1)S(1)}, u32[]{:S(2)}, u32[]{:S(2)}) collective-permute-start(bf16[256,2176]{1,0:T(8,128)(2,1)S(1)} %collective-permute-done.4), channel_id=1, source_target_pairs={{1,3},{3,1},{4,6},{6,4},{9,11},{11,9},{12,14},{14,12},{17,19},{19,... | collective-permute-start | bytes 3342344 | tf_op jit(solution)/shard_map/ppermute | solution.py:84
  122.8 11.4 %collective-permute-start.14 = (bf16[256,2176]{1,0:T(8,128)(2,1)S(1)}, bf16[256,2176]{1,0:T(8,128)(2,1)S(1)}, u32[]{:S(2)}, u32[]{:S(2)}) collective-permute-start(bf16[256,2176]{1,0:T(8,128)(2,1)S(1)} %collective-permute-done.3), channel_id=1, source_target_pairs={{1,3},{3,1},{4,6},{6,4},{9,11},{11,9},{12,14},{14,12},{17,19},{19,... | collective-permute-start | bytes 3342344 | tf_op jit(solution)/shard_map/ppermute | solution.py:84
  124.0 52.7 %copy-start.2 = (bf16[1024,2176]{1,0:T(8,128)(2,1)}, bf16[1024,2176]{1,0:T(8,128)(2,1)S(1)}, u32[]{:S(2)}) copy-start(bf16[1024,2176]{1,0:T(8,128)(2,1)S(1)} %select_dynamic-update-slice_fusion.4) | copy-start | bytes 13369348
  132.9 43.7 %copy-start = (f32[1024,2176]{1,0:T(8,128)}, f32[1024,2176]{1,0:T(8,128)S(1)}, u32[]{:S(2)}) copy-start(f32[1024,2176]{1,0:T(8,128)S(1)} %convolution_multiply_fusion) | copy-start | bytes 26738692
  133.0 24.2 %collective-permute-start.13 = (bf16[256,2176]{1,0:T(8,128)(2,1)S(1)}, bf16[256,2176]{1,0:T(8,128)(2,1)S(1)}, u32[]{:S(2)}, u32[]{:S(2)}) collective-permute-start(bf16[256,2176]{1,0:T(8,128)(2,1)S(1)} %collective-permute-done.12), channel_id=1, source_target_pairs={{1,8},{3,10},{9,16},{11,18},{12,5},{14,7},{17,24},{19,26},{20,13},... | collective-permute-start | bytes 3342344 | tf_op jit(solution)/shard_map/ppermute | solution.py:84
  134.3 34.8 %collective-permute-start.15 = (bf16[256,2176]{1,0:T(8,128)(2,1)S(1)}, bf16[256,2176]{1,0:T(8,128)(2,1)S(1)}, u32[]{:S(2)}, u32[]{:S(2)}) collective-permute-start(bf16[256,2176]{1,0:T(8,128)(2,1)S(1)} %collective-permute-done.14), channel_id=1, source_target_pairs={{1,8},{3,10},{9,16},{11,18},{12,5},{14,7},{17,24},{19,26},{20,13},... | collective-permute-start | bytes 3342344 | tf_op jit(solution)/shard_map/ppermute | solution.py:84
  174.5 3.5 %copy-start.1 = (f32[1024,2176]{1,0:T(8,128)}, f32[1024,2176]{1,0:T(8,128)S(1)}, u32[]{:S(2)}) copy-start(f32[1024,2176]{1,0:T(8,128)S(1)} %convolution_multiply_fusion.1) | copy-start | bytes 26738692
  178.0 5.8 %copy-start.3 = (bf16[1024,1024]{1,0:T(8,128)(2,1)}, bf16[1024,1024]{1,0:T(8,128)(2,1)S(1)}, u32[]{:S(2)}) copy-start(bf16[1024,1024]{1,0:T(8,128)(2,1)S(1)} %get-tuple-element.12) | copy-start | bytes 6291460
  178.0 5.8 %copy-start.5 = (bf16[1024,1024]{1,0:T(8,128)(2,1)}, bf16[1024,1024]{1,0:T(8,128)(2,1)S(1)}, u32[]{:S(2)}) copy-start(bf16[1024,1024]{1,0:T(8,128)(2,1)S(1)} %get-tuple-element.10) | copy-start | bytes 6291460
  183.8 4.9 %collective-permute-start.23 = (bf16[1024,1152]{1,0:T(8,128)(2,1)}, bf16[1024,1152]{1,0:T(8,128)(2,1)}, u32[]{:S(2)}, u32[]{:S(2)}) collective-permute-start(bf16[1024,1152]{1,0:T(8,128)(2,1)} %subtract_convert_fusion), channel_id=1, source_target_pairs={{0,1},{1,0},{2,3},{3,2},{4,5},{5,4},{6,7},{7,6},{8,9},{9,8},{10,11... | collective-permute-start | bytes 7077896 | tf_op jit(solution)/shard_map/ppermute | solution.py:84
  183.8 30.5 %collective-permute-start.18 = (bf16[1024,1152]{1,0:T(8,128)(2,1)}, bf16[1024,1152]{1,0:T(8,128)(2,1)}, u32[]{:S(2)}, u32[]{:S(2)}) collective-permute-start(bf16[1024,1152]{1,0:T(8,128)(2,1)} %subtract_convert_fusion), channel_id=1, source_target_pairs={{1,8},{3,10},{5,12},{7,14},{8,1},{9,16},{10,3},{11,18},{12,5},{13,... | collective-permute-start | bytes 7077896 | tf_op jit(solution)/shard_map/ppermute | solution.py:84
  186.0 28.3 %copy-start.4 = (bf16[1024,1024]{1,0:T(8,128)(2,1)S(1)}, bf16[1024,1024]{1,0:T(8,128)(2,1)}, u32[]{:S(2)}) copy-start(bf16[1024,1024]{1,0:T(8,128)(2,1)} %copy-done.3) | copy-start | bytes 6291460
  221.4 6.7 %collective-permute-start.32 = (f32[256,128]{1,0:T(8,128)S(1)}, f32[256,128]{1,0:T(8,128)S(1)}, u32[]{:S(2)}, u32[]{:S(2)}) collective-permute-start(f32[256,128]{1,0:T(8,128)S(1)} %get-tuple-element.31), channel_id=1, source_target_pairs={{0,0},{1,4},{2,2},{3,6},{4,1},{5,5},{6,3},{7,7},{8,8},{9,12},{10,1... | collective-permute-start | bytes 393224 | tf_op jit(solution)/shard_map/ppermute | solution.py:84
  222.0 7.7 %collective-permute-start.33 = (f32[256,128]{1,0:T(8,128)S(1)}, f32[256,128]{1,0:T(8,128)S(1)}, u32[]{:S(2)}, u32[]{:S(2)}) collective-permute-start(f32[256,128]{1,0:T(8,128)S(1)} %get-tuple-element.30), channel_id=1, source_target_pairs={{0,1},{1,5},{2,3},{3,7},{4,0},{5,4},{6,2},{7,6},{8,9},{9,13},{10,1... | collective-permute-start | bytes 393224 | tf_op jit(solution)/shard_map/ppermute | solution.py:84
  224.9 48.9 %collective-permute-start.28 = (bf16[256,512]{1,0:T(8,128)(2,1)S(1)}, bf16[256,512]{1,0:T(8,128)(2,1)S(1)}, u32[]{:S(2)}, u32[]{:S(2)}) collective-permute-start(bf16[256,512]{1,0:T(8,128)(2,1)S(1)} %get-tuple-element.21), channel_id=1, source_target_pairs={{0,0},{1,4},{2,2},{3,6},{4,1},{5,5},{6,3},{7,7},{8,8},{9,12},{10,1... | collective-permute-start | bytes 786440 | tf_op jit(solution)/shard_map/ppermute | solution.py:84
  225.6 48.3 %collective-permute-start.29 = (bf16[256,512]{1,0:T(8,128)(2,1)S(1)}, bf16[256,512]{1,0:T(8,128)(2,1)S(1)}, u32[]{:S(2)}, u32[]{:S(2)}) collective-permute-start(bf16[256,512]{1,0:T(8,128)(2,1)S(1)} %get-tuple-element.20), channel_id=1, source_target_pairs={{0,1},{1,5},{2,3},{3,7},{4,0},{5,4},{6,2},{7,6},{8,9},{9,13},{10,1... | collective-permute-start | bytes 786440 | tf_op jit(solution)/shard_map/ppermute | solution.py:84
  227.6 46.4 %collective-permute-start.30 = (bf16[256,512]{1,0:T(8,128)(2,1)S(1)}, bf16[256,512]{1,0:T(8,128)(2,1)S(1)}, u32[]{:S(2)}, u32[]{:S(2)}) collective-permute-start(bf16[256,512]{1,0:T(8,128)(2,1)S(1)} %get-tuple-element.19), channel_id=1, source_target_pairs={{0,2},{1,6},{2,0},{3,4},{4,3},{5,7},{6,1},{7,5},{8,10},{9,14},{10,... | collective-permute-start | bytes 786440 | tf_op jit(solution)/shard_map/ppermute | solution.py:84
  228.1 3.3 %collective-permute-start.19 = (bf16[256,512]{1,0:T(8,128)(2,1)S(1)}, bf16[256,512]{1,0:T(8,128)(2,1)S(1)}, u32[]{:S(2)}, u32[]{:S(2)}) collective-permute-start(bf16[256,512]{1,0:T(8,128)(2,1)S(1)} %get-tuple-element.29), channel_id=1, source_target_pairs={{0,0},{1,4},{2,2},{3,6},{4,1},{5,5},{6,3},{7,7},{8,8},{9,12},{10,1... | collective-permute-start | bytes 786440 | tf_op jit(solution)/shard_map/ppermute | solution.py:84
  229.7 14.3 %collective-permute-start.20 = (bf16[256,512]{1,0:T(8,128)(2,1)S(1)}, bf16[256,512]{1,0:T(8,128)(2,1)S(1)}, u32[]{:S(2)}, u32[]{:S(2)}) collective-permute-start(bf16[256,512]{1,0:T(8,128)(2,1)S(1)} %get-tuple-element.28), channel_id=1, source_target_pairs={{0,1},{1,5},{2,3},{3,7},{4,0},{5,4},{6,2},{7,6},{8,9},{9,13},{10,1... | collective-permute-start | bytes 786440 | tf_op jit(solution)/shard_map/ppermute | solution.py:84
  231.3 42.4 %copy-start.8 = (f32[2,256,128]{2,1,0:T(8,128)}, f32[2,256,128]{2,1,0:T(8,128)S(1)}, u32[]{:S(2)}) copy-start(f32[2,256,128]{2,1,0:T(8,128)S(1)} %bitcast_dynamic-update-slice_fusion.12) | copy-start | bytes 786436
  231.4 12.7 %collective-permute-start.21 = (bf16[256,512]{1,0:T(8,128)(2,1)S(1)}, bf16[256,512]{1,0:T(8,128)(2,1)S(1)}, u32[]{:S(2)}, u32[]{:S(2)}) collective-permute-start(bf16[256,512]{1,0:T(8,128)(2,1)S(1)} %get-tuple-element.27), channel_id=1, source_target_pairs={{0,2},{1,6},{2,0},{3,4},{4,3},{5,7},{6,1},{7,5},{8,10},{9,14},{10,... | collective-permute-start | bytes 786440 | tf_op jit(solution)/shard_map/ppermute | solution.py:84
  244.0 9.5 %collective-permute-start.22 = (bf16[256,512]{1,0:T(8,128)(2,1)S(1)}, bf16[256,512]{1,0:T(8,128)(2,1)S(1)}, u32[]{:S(2)}, u32[]{:S(2)}) collective-permute-start(bf16[256,512]{1,0:T(8,128)(2,1)S(1)} %get-tuple-element.26), channel_id=1, source_target_pairs={{0,3},{1,7},{2,1},{3,5},{4,2},{5,6},{6,0},{7,4},{8,11},{9,15},{10,... | collective-permute-start | bytes 786440 | tf_op jit(solution)/shard_map/ppermute | solution.py:84
  244.1 9.5 %collective-permute-start.24 = (bf16[256,512]{1,0:T(8,128)(2,1)S(1)}, bf16[256,512]{1,0:T(8,128)(2,1)S(1)}, u32[]{:S(2)}, u32[]{:S(2)}) collective-permute-start(bf16[256,512]{1,0:T(8,128)(2,1)S(1)} %get-tuple-element.25), channel_id=1, source_target_pairs={{0,0},{1,4},{2,2},{3,6},{4,1},{5,5},{6,3},{7,7},{8,8},{9,12},{10,1... | collective-permute-start | bytes 786440 | tf_op jit(solution)/shard_map/ppermute | solution.py:84
  253.5 6.8 %collective-permute-start.25 = (bf16[256,512]{1,0:T(8,128)(2,1)S(1)}, bf16[256,512]{1,0:T(8,128)(2,1)S(1)}, u32[]{:S(2)}, u32[]{:S(2)}) collective-permute-start(bf16[256,512]{1,0:T(8,128)(2,1)S(1)} %get-tuple-element.24), channel_id=1, source_target_pairs={{0,1},{1,5},{2,3},{3,7},{4,0},{5,4},{6,2},{7,6},{8,9},{9,13},{10,1... | collective-permute-start | bytes 786440 | tf_op jit(solution)/shard_map/ppermute | solution.py:84
  253.6 6.8 %collective-permute-start.26 = (bf16[256,512]{1,0:T(8,128)(2,1)S(1)}, bf16[256,512]{1,0:T(8,128)(2,1)S(1)}, u32[]{:S(2)}, u32[]{:S(2)}) collective-permute-start(bf16[256,512]{1,0:T(8,128)(2,1)S(1)} %get-tuple-element.23), channel_id=1, source_target_pairs={{0,2},{1,6},{2,0},{3,4},{4,3},{5,7},{6,1},{7,5},{8,10},{9,14},{10,... | collective-permute-start | bytes 786440 | tf_op jit(solution)/shard_map/ppermute | solution.py:84
  260.3 11.9 %collective-permute-start.27 = (bf16[256,512]{1,0:T(8,128)(2,1)S(1)}, bf16[256,512]{1,0:T(8,128)(2,1)S(1)}, u32[]{:S(2)}, u32[]{:S(2)}) collective-permute-start(bf16[256,512]{1,0:T(8,128)(2,1)S(1)} %get-tuple-element.22), channel_id=1, source_target_pairs={{0,3},{1,7},{2,1},{3,5},{4,2},{5,6},{6,0},{7,4},{8,11},{9,15},{10,... | collective-permute-start | bytes 786440 | tf_op jit(solution)/shard_map/ppermute | solution.py:84
  260.4 15.4 %collective-permute-start.31 = (bf16[256,512]{1,0:T(8,128)(2,1)S(1)}, bf16[256,512]{1,0:T(8,128)(2,1)S(1)}, u32[]{:S(2)}, u32[]{:S(2)}) collective-permute-start(bf16[256,512]{1,0:T(8,128)(2,1)S(1)} %get-tuple-element.18), channel_id=1, source_target_pairs={{0,3},{1,7},{2,1},{3,5},{4,2},{5,6},{6,0},{7,4},{8,11},{9,15},{10,... | collective-permute-start | bytes 786440 | tf_op jit(solution)/shard_map/ppermute | solution.py:84
  275.8 1.0 copy-start.6

commit v2 on v1

v2 whole, which is shorter than its diff:
```python
import jax
import jax.numpy as jnp
from jax import lax
from jax.experimental import pallas as pl
from jax.experimental.pallas import tpu as pltpu
from jax.sharding import PartitionSpec as P

AXES = ("tm", "row")
LANES = 128


def from_behind(array, axis, by):
    count = lax.axis_size(axis)
    pairs = [(i, i + by) for i in range(count) if 0 <= i + by < count]
    return lax.ppermute(array, axis, pairs)


def stacked(left_blocks, right_blocks):
    return jnp.einsum("bij,bjk->bik", left_blocks, right_blocks, preferred_element_type=jnp.float32)


def neighbour_terms(lower_rows, upper_rows, panel_rows, distance):
    below_in = from_behind(panel_rows[-distance:], "tm", 1)
    above_in = from_behind(panel_rows[:distance], "tm", -1)
    below_panel = jnp.concatenate([below_in, panel_rows[:-distance]], axis=0)
    above_panel = jnp.concatenate([panel_rows[distance:], above_in], axis=0)
    below_full = lax.all_gather(below_panel, "row", axis=1, tiled=True)
    above_full = lax.all_gather(above_panel, "row", axis=1, tiled=True)
    return (stacked(lower_rows, below_full), stacked(upper_rows, above_full))


def apply_terms(below_term, above_term, excess_rows, rhs_rows, states):
    lower_new = (-below_term[:, :, :states]).astype(jnp.bfloat16)
    upper_new = (-above_term[:, :, states : 2 * states]).astype(jnp.bfloat16)
    excess_new = (
        excess_rows - below_term[:, :, states : 2 * states] - above_term[:, :, :states]
    ).astype(jnp.bfloat16)
    rhs_new = rhs_rows - below_term[:, :, 2 * states :] - above_term[:, :, 2 * states :]
    return (lower_new, upper_new, excess_new, rhs_new)


def shards_by_rows(lower, upper, shift_diag, rhs):
    groups, height, states = lower.shape
    offset = lax.axis_index("row") * height
    columns = lax.broadcasted_iota(jnp.int32, (groups, height, states), 2)
    row_pos = lax.broadcasted_iota(jnp.int32, (groups, height, states), 1) + offset
    excess_zero = jnp.where(columns == row_pos, shift_diag[:, :, None], 0.0)
    panel_one = scaled_panel(lower, upper, shift_diag, rhs)
    below_one, above_one = neighbour_terms(lower, upper, panel_one, 1)
    lower_one, upper_one, excess_one, rhs_one = apply_terms(
        below_one, above_one, excess_zero, rhs, states
    )
    own_rows = jnp.concatenate([lower_one, upper_one, rhs_one.astype(jnp.bfloat16)], axis=2)
    product = stacked(excess_one, lax.all_gather(own_rows, "row", axis=1, tiled=True))
    panel_two = (own_rows.astype(jnp.float32) - product).astype(jnp.bfloat16)
    below_two, above_two = neighbour_terms(lower_one, upper_one, panel_two, 2)
    return apply_terms(below_two, above_two, excess_one.astype(jnp.float32), rhs_one, states)


def scaled_panel(lower, upper, shift_diag, rhs):
    scaling = (1.0 - shift_diag)[..., None]
    parts = [lower.astype(jnp.float32), upper.astype(jnp.float32), rhs]
    return (scaling * jnp.concatenate(parts, axis=-1)).astype(jnp.bfloat16)


def dot(left, right):
    return jnp.dot(left, right, preferred_element_type=jnp.float32)


def call(kernel, outs, *arrays, scratch=(), **grid):
    if not grid:
        grid = dict(
            in_specs=[whole(array.shape) for array in arrays[1:]],
            out_specs=[whole(out.shape) for out in outs],
            grid=(1,),
        )
    return pl.pallas_call(
        kernel,
        out_shape=outs,
        grid_spec=pltpu.PrefetchScalarGridSpec(
            num_scalar_prefetch=1, scratch_shapes=list(scratch), **grid
        ),
        compiler_params=pltpu.CompilerParams(vmem_limit_bytes=32 << 20),
    )(*arrays)


def whole(shape):
    return pl.BlockSpec(shape, lambda *_: (0,) * len(shape))


def shaped(shape, dtype=jnp.bfloat16):
    return jax.ShapeDtypeStruct(shape, dtype)


def pack(place, lower, upper, shift_diag, rhs):
    height, states = lower.shape[1:]
    scenarios = rhs.shape[2]
    width = 2 * states + scenarios
    rows = height // 2

    def kernel(place_ref, lower_ref, upper_ref, shift_ref, rhs_ref, outer, inner_all, first, second):
        y, home = place_ref[1], place_ref[4]
        across = lax.broadcasted_iota(jnp.int32, (rows, height), 1)
        down = lax.broadcasted_iota(jnp.int32, (rows, height), 0) + pl.program_id(0) * rows

        lane = lax.broadcasted_iota(jnp.int32, (rows, LANES), 1)

        def panel(block, *outs):
            shift = jnp.broadcast_to(shift_ref[pl.ds(block, 1), :], (rows, height))
            shift = jnp.sum(jnp.where(across == down, shift, 0.0), axis=1, keepdims=True)
            for at, ref in ((0, lower_ref), (states, upper_ref), (2 * states, rhs_ref)):
                part = ((1.0 - shift) * ref[block].astype(jnp.float32)).astype(jnp.bfloat16)
                for out in outs:
                    if out is not None:
                        out[:, at : at + part.shape[1]] = part
            tail = jnp.zeros((rows, LANES), jnp.float32)
            for index in range(3):
                part = shift.astype(jnp.bfloat16).astype(jnp.float32)
                tail = jnp.where(lane == index, part, tail)
                shift = shift - part
            for out in outs[1:]:
                out[:, width:] = tail.astype(jnp.bfloat16)

        @pl.when(home == 1)
        def _():
            panel(y, outer, second)
            panel(1 - y, None, inner_all, first)

        @pl.when(home == 0)
        def _():
            panel(y, outer, first)
            panel(1 - y, None, inner_all, second)

    def rows_of(array):
        return pl.BlockSpec((2, rows, array.shape[2]), lambda i, _: (0, i, 0))

    return call(
        kernel,
        [shaped((height, width))] + [shaped((height, width + LANES))] * 3,
        place, lower, upper, shift_diag, rhs,
        grid=(2,),
        in_specs=[rows_of(lower), rows_of(upper), whole(shift_diag.shape), rows_of(rhs)],
        out_specs=[pl.BlockSpec((rows, width), lambda i, _: (i, 0))]
        + [pl.BlockSpec((rows, width + LANES), lambda i, _: (i, 0))] * 3,
    )


def level_one(place, centre, near, far, scenarios):
    states = centre.shape[0]
    half, tile, chunk = states // 2, states // 4, states // 2
    steps = states // tile

    def kernel(
        place_ref, centre_ref, near_n, near_f, near_r, far_n, far_f, far_r,
        near_out, far_out, excess_out, rhs_out, panel_near, panel_rest, ones, excess_all,
    ):
        step = pl.program_id(0)
        k, x = place_ref[3], place_ref[2]
        near_at = pl.multiple_of((1 - k) * states, states)
        far_at = pl.multiple_of(k * states, states)
        here = pl.ds(pl.multiple_of(step * tile, tile), tile)
        for at in range(0, states, chunk):
            rows = slice(at, at + chunk)
            left_near = centre_ref[rows, pl.ds(near_at, states)]
            left_far = centre_ref[rows, pl.ds(far_at, states)]
            parts = centre_ref[rows, 2 * states + scenarios :].astype(jnp.float32)
            shift_rows = parts[:, 0:1] + parts[:, 1:2] + parts[:, 2:3]
            unscale = 1.0 / (1.0 - shift_rows)
            near_one = (-unscale * dot(left_near, near_n[...])).astype(jnp.bfloat16)
            near_out[rows, :] = near_one
            ones[0, rows, here] = near_one
            far_one = (-unscale * dot(left_far, far_f[...])).astype(jnp.bfloat16)
            far_out[rows, :] = far_one
            ones[1, rows, here] = far_one
            across = lax.broadcasted_iota(jnp.int32, (chunk, tile), 1) + step * tile
            down = lax.broadcasted_iota(jnp.int32, (chunk, tile), 0) + at
            cross = dot(left_near, near_f[...]) + dot(left_far, far_n[...])
            excess = jnp.where(across == down, shift_rows, 0.0) - unscale * cross
            excess = excess.astype(jnp.bfloat16)
            excess_out[rows, :] = excess
            excess_all[rows, here] = excess

            @pl.when(step == 0)
            def _():
                own = centre_ref[rows, 2 * states : 2 * states + scenarios].astype(jnp.float32)
                cross = dot(left_near, near_r[...]) + dot(left_far, far_r[...])
                rhs_out[rows, :] = unscale * (own - cross)

        @pl.when(step == steps - 1)
        def _():
            columns = pl.ds(pl.multiple_of(x * half, half), half)
            rhs_all = rhs_out[...].astype(jnp.bfloat16)
            for at in range(0, states, chunk):
                rows = slice(at, at + chunk)
                excess = excess_all[rows, :]

                def panel(own_all, own):
                    return (own.astype(jnp.float32) - dot(excess, own_all)).astype(jnp.bfloat16)

                panel_near[rows, :] = panel(ones[0, :, columns], ones[0, rows, columns])
                panel_rest[rows, :half] = panel(ones[1, :, columns], ones[1, rows, columns])
                panel_rest[rows, half:] = panel(rhs_all, rhs_all[rows, :])

    def side(flipped):
        def at(step, place_ref):
            k = place_ref[3]
            return (0, (k if flipped else 1 - k) * steps + step)

        return pl.BlockSpec((states, tile), at)

    rest = pl.BlockSpec((states, scenarios), lambda *_: (0, 2 * states // scenarios))
    blocks = pl.BlockSpec((states, tile), lambda step, _: (0, step))
    square = shaped((states, states))
    outs = [square, square, square, shaped((states, scenarios), jnp.float32),
            shaped((states, half)), shaped((states, half + scenarios))]
    return call(
        kernel,
        outs,
        place, centre, near, near, near, far, far, far,
        scratch=[pltpu.VMEM((2, states, states), jnp.bfloat16),
                 pltpu.VMEM((states, states), jnp.bfloat16)],
        grid=(steps,),
        in_specs=[pl.BlockSpec(centre.shape, lambda *_: (0, 0), pipeline_mode=pl.Buffered(1)),
                  side(False), side(True), rest, side(False), side(True), rest],
        out_specs=[blocks] * 3 + [whole(out.shape) for out in outs[3:]],
    )


def message_rows(place_ref, states, message):
    quarter = states // 4
    at = (place_ref[2] ^ (message // 2)) * 2 + (place_ref[1] ^ (message % 2))
    return pl.ds(pl.multiple_of(at * quarter, quarter), quarter)


def messages(place, left, right, width):
    states = left.shape[0]

    def kernel(place_ref, left_ref, right_ref, *outs):
        for message, out in enumerate(outs):
            rows = message_rows(place_ref, states, message)
            out[...] = (-dot(left_ref[rows, :], right_ref[...])).astype(jnp.bfloat16)

    outs = [shaped((states // 4, width))] * 4
    return call(
        kernel, outs, place, left, right,
        grid=(1,),
        in_specs=[whole(left.shape), pl.BlockSpec((states, width), lambda *_: (0, 0))],
        out_specs=[whole(out.shape) for out in outs],
    )


def near_rest(place, left, near, rest, excess, rhs):
    states, half = near.shape
    scenarios = rhs.shape[1]

    def kernel(place_ref, left_ref, near_ref, rest_ref, excess_ref, rhs_ref, excess_out, rhs_out):
        excess_out[...] = excess_ref[...].astype(jnp.float32) - dot(left_ref[...], near_ref[...])
        rhs_out[...] = rhs_ref[...] - dot(left_ref[...], rest_ref[...])

    rows = states // 4

    def by_rows(width, at=lambda place_ref: 0):
        return pl.BlockSpec((rows, width), lambda i, place_ref: (i, at(place_ref)))

    return call(
        kernel,
        [shaped((states, half), jnp.float32), shaped((states, scenarios), jnp.float32)],
        place, left, near, rest, excess, rhs,
        grid=(4,),
        in_specs=[by_rows(states), whole(near.shape),
                  pl.BlockSpec((states, scenarios), lambda *_: (0, half // scenarios)),
                  by_rows(half, lambda place_ref: place_ref[2]), by_rows(scenarios)],
        out_specs=[by_rows(half), by_rows(scenarios)],
    )


def far_rest(place, left, rest, excess, rhs):
    states, half = excess.shape
    scenarios = rhs.shape[1]

    def kernel(place_ref, left_ref, rest_ref, excess_ref, rhs_ref, *outs):
        for message in range(4):
            rows = message_rows(place_ref, states, message)
            product = dot(left_ref[rows, :], rest_ref[:, :half])
            outs[message][...] = (excess_ref[rows, :] - product).astype(jnp.bfloat16)
            if message < 2:
                product = dot(left_ref[rows, :], rest_ref[:, half:])
                outs[4 + message][...] = rhs_ref[rows, :] - product

    quarter = states // 4
    outs = [shaped((quarter, half))] * 4 + [shaped((quarter, scenarios), jnp.float32)] * 2
    return call(kernel, outs, place, left, rest, excess, rhs)


def after(array, *others):
    return lax.optimization_barrier((array, others))[0]


def shards_by_blocks(lower, upper, shift_diag, rhs):
    height, states = lower.shape[1:]
    scenarios = rhs.shape[2]
    half = states // 2
    planes = lax.axis_size("tm") // 2
    group, row = lax.axis_index("tm"), lax.axis_index("row")
    y, z, x, k = group % 2, group // 2, row // 2, row % 2
    home = k == y
    place = jnp.stack([z, y, x, k, home.astype(jnp.int32)])

    def send(array, to):
        pairs = []
        for device in range(planes * 8):
            gz, gy, gx, gk = device // 8, device // 4 % 2, device // 2 % 2, device % 2
            target = to(gx, gy, gz, gk)
            if target is not None and 0 <= target[2] < planes:
                tx, ty, tz, tk = target
                pairs.append((device, tz * 8 + ty * 4 + tx * 2 + tk))
        return lax.ppermute(array, AXES, pairs)

    def swap(array):
        return send(array, lambda x, y, z, k: (x, y, z, 1 - k))

    def across_x(array):
        return send(array, lambda x, y, z, k: (1 - x, y, z, k))

    def away_x(array):
        return send(array, lambda x, y, z, k: (1 - x, y, z, k) if k != y else None)

    def away_to_home_z(array):
        return send(array, lambda x, y, z, k: (x, y, z + 1 - 2 * y, y) if k != y else None)

    outer, inner, first, second = pack(place, lower, upper, shift_diag, rhs)

    far_a = send(outer, lambda x, y, z, k: (x, 1 - y, z, y) if k == y else None)
    far_b = send(outer, lambda x, y, z, k: (x, 1 - y, z, y) if k != y else None)
    inner_x = across_x(inner)
    inner_k = swap(inner)
    centre_a = send(
        after(first, far_a), lambda x, y, z, k: (x, 1 - y, z, y) if k == y else (x, y, z, y)
    )
    far_xa, halo_b = away_x(far_a), away_to_home_z(far_a)
    centre_b = send(
        after(second, far_b), lambda x, y, z, k: (x, y, z, y) if k == y else (x, 1 - y, z, y)
    )
    far_xb, halo_a = away_x(far_b), away_to_home_z(far_b)
    inner_xk = swap(inner_x)
    first_x = after(jnp.where(home, second, inner_x), centre_a, far_xa)
    second_x = after(jnp.where(home, inner_x, first), centre_b, far_xb)
    centre_xa = send(
        first_x, lambda x, y, z, k: (1 - x, y, z, y) if k == y else (x, 1 - y, z, y)
    )
    halo_xb = away_to_home_z(far_xa)
    centre_xb = send(
        second_x, lambda x, y, z, k: (x, 1 - y, z, y) if k == y else (1 - x, y, z, y)
    )
    halo_xa = away_to_home_z(far_xb)

    def assembled(*pieces):
        panel = jnp.zeros((states, pieces[0][0].shape[1]), jnp.bfloat16)
        for piece, px, pk in pieces:
            panel = lax.dynamic_update_slice_in_dim(panel, piece, px * half + pk * height, 0)
        return panel

    def pick(at_home, away):
        return jnp.where(home, at_home, away)

    near = assembled(
        (inner, x, k), (inner_k, x, 1 - k), (inner_x, 1 - x, k), (inner_xk, 1 - x, 1 - k)
    )
    far = assembled(
        (pick(halo_a, far_a), x, k), (pick(halo_b, far_b), x, 1 - k),
        (pick(halo_xa, far_xa), 1 - x, k), (pick(halo_xb, far_xb), 1 - x, 1 - k),
    )
    centre = assembled(
        (centre_b, x, y), (centre_a, x, 1 - y), (centre_xa, 1 - x, y), (centre_xb, 1 - x, 1 - y)
    )

    near_one, far_one, excess_one, rhs_one, panel_near, panel_rest = level_one(
        place, centre, near, far, scenarios
    )

    def across_z(array):
        return send(array, lambda x, y, z, k: (x, y, z - 1 + 2 * k, 1 - k))

    def at_home(pieces):
        return [
            (send(piece, lambda x, y, z, k, m=m: (x ^ (m // 2), k, z, y ^ (m % 2))), m)
            for m, piece in enumerate(pieces)
        ]

    far_two_near = across_z(panel_near)
    near_two_rest = swap(panel_rest)
    near_new = messages(place, near_one, near_two_rest, half)
    near_two_near = swap(panel_near)
    far_two_rest = across_z(after(panel_rest, near_two_rest))
    near_home = at_home(near_new)
    excess_part, rhs_part = near_rest(
        place, near_one, near_two_near, near_two_rest, excess_one, rhs_one
    )
    far_two_near = after(far_two_near, near_new, excess_part)
    far_home = at_home(messages(place, far_one, far_two_near, half))
    last = far_rest(place, far_one, far_two_rest, excess_part, rhs_part)
    excess_home = at_home(last[:4])
    rhs_home = at_home(last[4:])

    def placed(pieces, width, dtype):
        result = jnp.zeros((2, height, width), dtype)
        for piece, m in pieces:
            start = (k ^ (m % 2), 0, (x ^ (m // 2)) * half if len(pieces) > 2 else 0)
            result = lax.dynamic_update_slice(result, piece[None], start)
        return result

    def chosen(ours, theirs):
        return [(jnp.where(y == 0, a, b), m) for (a, m), (b, _) in zip(ours, theirs)]

    lower_two = placed(chosen(far_home, near_home), states, jnp.bfloat16)
    upper_two = placed(chosen(near_home, far_home), states, jnp.bfloat16)
    excess_two = placed(excess_home, states, jnp.bfloat16)
    rhs_two = placed(rhs_home, scenarios, jnp.float32)
    return lower_two, upper_two, excess_two, rhs_two


def solution(mesh):
    paired = mesh.shape["row"] == 4 and mesh.shape["tm"] % 2 == 0
    spec = P("tm", "row", None)

    def program(lower, upper, shift_diag, rhs):
        two_blocks = lower.shape[0] == 2 * mesh.shape["tm"]
        return jax.shard_map(
            shards_by_blocks if paired and two_blocks else shards_by_rows,
            mesh=mesh,
            in_specs=(spec, spec, P("tm", "row"), spec),
            out_specs=(spec,) * 4,
            check_vma=False,
        )(lower, upper, shift_diag, rhs)

    return program
```

time: 279 us -> 197 us (0.71)
  blocking collectives: 37.9 us -> 0 us
  waiting for transfers between devices: 133 us -> 98.7 us
  Pallas kernels: 0 us -> 30.6 us
  matrix products: 29 us -> 0 us
  other arithmetic: 17.3 us -> 6.09 us
    all_gather x1 -> x0, blocking collectives: 37.9 us -> none  [shards_by_blocks(): shifts = lax.all_gather(shift_diag, AXES, axis=0, tiled=False)]
    ppermute x34 -> x33, waiting for transfers between devices: 133 us -> 98.7 us  [send(): return lax.ppermute(array, AXES, pairs)]
    pallas_call x0 -> x6, Pallas kernels: none -> 30.6 us  [call(): pl.pallas_call(kernel, out_shape=outs, grid_spec=pltpu.PrefetchScalarGrid...]
    dot_general x5 -> x0, matrix products: 29 us -> none  [dot(): return jnp.dot(left, right, preferred_element_type=jnp.float32)]
    convert_element_type x6 -> x0, other arithmetic: 11.4 us -> none  [the longest x2 5.65 us: scaled_panel(): parts = [lower.astype(jnp.float32), upper.astype(jnp.float32), rhs]]
    unnamed x20 -> x42, local copies, waits for them, and re-layouts: 2.38 us -> 8.61 us
    dynamic_update_slice x4 -> x7, local copies, waits for them, and re-layouts: 7.26 us -> 2.08 us  [assembled(): lax.dynamic_update_slice_in_dim(panel, piece, px * half + pk * height, 0)]
    ppermute x34 -> x33, starting transfers between devices: 44.6 us -> 46.8 us  [send(): return lax.ppermute(array, AXES, pairs)]
  transfers between devices with their start and end apart: 34 -> 33, of which waited for: 14 -> 13; matrix products, arithmetic and copies ran while one was open for 9% -> 5% of each run, Pallas kernels for 0% -> 5%
where the time goes in v2:
time: 197 us; the launch traced here: 196 us
  waiting for transfers between devices  98.7 us (50%)
  starting transfers between devices  46.8 us (24%)
  Pallas kernels  30.6 us (16%)
  local copies, waits for them, and re-layouts  12.2 us (6%)
  other arithmetic  6.09 us (3%)
    ppermute x33, waiting for transfers between devices, send(): return lax.ppermute(array, AXES, pairs)  98.7 us
    ppermute x33, starting transfers between devices, send(): return lax.ppermute(array, AXES, pairs)  46.8 us
    pallas_call x6, Pallas kernels, call(): pl.pallas_call(kernel, out_shape=outs, grid_spec=pltpu.PrefetchScalarGrid...  30.6 us
    unnamed x42, local copies, waits for them, and re-layouts  8.61 us
  transfers between devices with their start and end apart: 33, of which 13 were waited for; matrix products, arithmetic and copies ran while one was open for 5% of the time, Pallas kernels for 5%

profile of v2, /device:TPU:8, one launch (start us, length us, event | category | flops | bytes accessed | tf_op | source)
XLA Modules:
  0.0 195.7 jit_solution(15736800637917497440)
XLA Ops:
  0.8 1.2 copy-done.2
  2.0 1.2 copy-done.3
  3.2 0.9 copy-done.6
  4.2 0.7 copy-done.7
  4.8 2.2 %shard_map.75 = (bf16[256,2176]{1,0:T(8,128)(2,1)}, bf16[256,2304]{1,0:T(8,128)(2,1)S(1)}, bf16[256,2304]{1,0:T(8,128)(2,1)S(1)}, bf16[256,2304]{1,0:T(8,128)(2,1)S(1)}) custom-call(s32[5]{0:T(128)S(1)} %stack.27.place_ref, bf16[2,256,1024]{2,1,0:T(8,128)(2,1)S(1)} %copy-done.2, bf16[2,256,1024]{2,1,0:T(8,128)(2,1)S(1)} %copy-done.3, ...), custom_call_target="tpu_custom_call" | custom-call | tf_op jit(solution)/shard_map/pallas_call | solution.py:77
  7.0 1.7 collective-permute-start
  8.7 5.3 %collective-permute-start.2 = (bf16[256,2176]{1,0:T(8,128)(2,1)}, bf16[256,2176]{1,0:T(8,128)(2,1)}, u32[]{:S(2)}, u32[]{:S(2)}) collective-permute-start(bf16[256,2176]{1,0:T(8,128)(2,1)} %get-tuple-element.37), channel_id=1, source_target_pairs={{0,4},{2,6},{5,1},{7,3},{8,12},{10,14},{13,9},{15,11},{16,20},{18,... | collective-permute-start | bytes 3342344 | tf_op jit(solution)/shard_map/ppermute | solution.py:317
  14.0 1.5 collective-permute-start.4
  15.5 0.3 broadcast.11.clone.1
  15.9 0.7 collective-permute-start.1
  16.7 18.5 %collective-permute-done.2 = bf16[256,2176]{1,0:T(8,128)(2,1)} collective-permute-done((bf16[256,2176]{1,0:T(8,128)(2,1)}, bf16[256,2176]{1,0:T(8,128)(2,1)}, u32[]{:S(2)}, u32[]{:S(2)}) %collective-permute-start.2) | collective-permute-done | bytes 1114144 | tf_op jit(solution)/shard_map/ppermute | solution.py:317
  35.1 1.3 collective-permute-start.11
  36.4 1.3 collective-permute-start.12
  37.7 0.7 collective-permute-start.7
  38.5 1.4 constant_dynamic-update-slice_fusion.2
  39.9 0.7 collective-permute-start.5
  40.6 2.0 %constant_dynamic-update-slice_fusion.1 = (bf16[1024,2304]{1,0:T(8,128)(2,1)S(1)}, bf16[256,2304]{1,0:T(8,128)(2,1)S(1)}, bf16[256,2304]{1,0:T(8,128)(2,1)S(1)}) fusion(bf16[1024,2304]{1,0:T(8,128)(2,1)S(1)} %constant_dynamic-update-slice_fusion.2, bf16[256,2304]{1,0:T(8,128)(2,1)} %collective-permute-done.4, s32[]{:T(128)S(6)} %select_n.162, ...), kind=kLoop, calls=%fused_computation.21 | loop fusion | flops 1179648 | bytes 7077893 | tf_op jit(solution)/shard_map/dynamic_update_slice | solution.py:360
  42.6 9.5 %collective-permute-done.11 = bf16[256,2176]{1,0:T(8,128)(2,1)S(1)} collective-permute-done((bf16[256,2176]{1,0:T(8,128)(2,1)}, bf16[256,2176]{1,0:T(8,128)(2,1)S(1)}, u32[]{:S(2)}, u32[]{:S(2)}) %collective-permute-start.11) | collective-permute-done | bytes 1114144 | tf_op jit(solution)/shard_map/ppermute | solution.py:317
  52.2 0.4 collective-permute-start.3
  52.8 0.4 select_dynamic-update-slice_fusion.3
  53.2 10.9 %collective-permute-done.12 = bf16[256,2176]{1,0:T(8,128)(2,1)S(1)} collective-permute-done((bf16[256,2176]{1,0:T(8,128)(2,1)}, bf16[256,2176]{1,0:T(8,128)(2,1)S(1)}, u32[]{:S(2)}, u32[]{:S(2)}) %collective-permute-start.12) | collective-permute-done | bytes 1114144 | tf_op jit(solution)/shard_map/ppermute | solution.py:317
  64.1 1.3 collective-permute-start.13
  65.4 1.3 collective-permute-start.14
  66.7 0.4 select_dynamic-update-slice_fusion.2
  67.1 6.3 %collective-permute-start.8 = (bf16[256,2304]{1,0:T(8,128)(2,1)S(1)}, bf16[256,2304]{1,0:T(8,128)(2,1)S(1)}, u32[]{:S(2)}, u32[]{:S(2)}) collective-permute-start(bf16[256,2304]{1,0:T(8,128)(2,1)S(1)} %get-tuple-element.43), channel_id=1, source_target_pairs={{0,4},{1,2},{2,6},{3,0},{4,7},{5,1},{6,5},{7,3},{8,12},{9,10},{10,... | collective-permute-start | bytes 3538952 | tf_op jit(solution)/shard_map/ppermute | solution.py:317
  73.5 1.5 collective-permute-start.6
  75.0 0.3 broadcast.11.clone
  75.7 5.3 %collective-permute-done.13 = bf16[256,2176]{1,0:T(8,128)(2,1)S(1)} collective-permute-done((bf16[256,2176]{1,0:T(8,128)(2,1)S(1)}, bf16[256,2176]{1,0:T(8,128)(2,1)S(1)}, u32[]{:S(2)}, u32[]{:S(2)}) %collective-permute-start.13) | collective-permute-done | bytes 1114144 | tf_op jit(solution)/shard_map/ppermute | solution.py:317
  80.9 0.3 select_dynamic-update-slice_fusion.1
  81.3 11.6 %collective-permute-done.14 = bf16[256,2176]{1,0:T(8,128)(2,1)S(1)} collective-permute-done((bf16[256,2176]{1,0:T(8,128)(2,1)S(1)}, bf16[256,2176]{1,0:T(8,128)(2,1)S(1)}, u32[]{:S(2)}, u32[]{:S(2)}) %collective-permute-start.14) | collective-permute-done | bytes 1114144 | tf_op jit(solution)/shard_map/ppermute | solution.py:317
  92.8 0.3 select_dynamic-update-slice_fusion.far_n.far_f.far_r
  93.2 6.3 %collective-permute-done.6 = bf16[256,2304]{1,0:T(8,128)(2,1)S(1)} collective-permute-done((bf16[256,2304]{1,0:T(8,128)(2,1)S(1)}, bf16[256,2304]{1,0:T(8,128)(2,1)S(1)}, u32[]{:S(2)}, u32[]{:S(2)}) %collective-permute-start.6) | collective-permute-done | bytes 1179680 | tf_op jit(solution)/shard_map/ppermute | solution.py:317
  99.7 18.7 %shard_map.76 = (bf16[1024,1024]{1,0:T(8,128)(2,1)S(1)}, bf16[1024,1024]{1,0:T(8,128)(2,1)S(1)}, bf16[1024,1024]{1,0:T(8,128)(2,1)S(1)}, f32[1024,128]{1,0:T(8,1...) custom-call(s32[5]{0:T(128)S(1)} %stack.27.place_ref, ...), custom_call_target="tpu_custom_call" | custom-call | tf_op jit(solution)/shard_map/pallas_call | solution.py:77
  118.6 0.4 collective-permute-start.17
  119.0 2.1 %collective-permute-start.15 = (bf16[1024,512]{1,0:T(8,128)(2,1)S(1)}, bf16[1024,512]{1,0:T(8,128)(2,1)S(1)}, u32[]{:S(2)}, u32[]{:S(2)}) collective-permute-start(bf16[1024,512]{1,0:T(8,128)(2,1)S(1)} %get-tuple-element.45), channel_id=1, source_target_pairs={{1,8},{3,10},{5,12},{7,14},{8,1},{9,16},{10,3},{11,18},{12,5},{13,... | collective-permute-start | bytes 3145736 | tf_op jit(solution)/shard_map/ppermute | solution.py:317
  121.0 1.5 collective-permute-done.16.right_ref.rest_ref
  122.5 2.0 %collective-permute-start.26 = (bf16[1024,640]{1,0:T(8,128)(2,1)}, bf16[1024,640]{1,0:T(8,128)(2,1)S(1)}, u32[]{:S(2)}, u32[]{:S(2)}) collective-permute-start(bf16[1024,640]{1,0:T(8,128)(2,1)} %get-tuple-element.60), channel_id=1, source_target_pairs={{1,8},{3,10},{5,12},{7,14},{8,1},{9,16},{10,3},{11,18},{12,5},{13,... | collective-permute-start | bytes 3932168 | tf_op jit(solution)/shard_map/ppermute | solution.py:317
  124.5 2.3 %shard_map.77 = (bf16[256,512]{1,0:T(8,128)(2,1)}, bf16[256,512]{1,0:T(8,128)(2,1)S(1)}, bf16[256,512]{1,0:T(8,128)(2,1)S(1)}, bf16[256,512]{1,0:T(8,128)(2,1)S(1)}) custom-call(s32[5]{0:T(128)S(1)} %stack.27.place_ref, bf16[1024,1024]{1,0:T(8,128)(2,1)S(1)} %get-tuple-element.46.left_ref, bf16[1024,640]{1,0:T(8,128)(2,1)S(1)} %collective-permute-done.16.right_ref.rest_ref), custom_call_target="tpu_custom_call" | custom-call | tf_op jit(solution)/shard_map/pallas_call | solution.py:77
  126.8 0.7 copy-done.12
  127.5 0.7 copy-done.13
  128.3 3.1 %shard_map.78 = (f32[1024,512]{1,0:T(8,128)S(1)}, f32[1024,128]{1,0:T(8,128)S(1)}) custom-call(s32[5]{0:T(128)S(1)} %stack.27.place_ref, bf16[1024,1024]{1,0:T(8,128)(2,1)S(1)} %get-tuple-element.46.left_ref, bf16[1024,512]{1,0:T(8,128)(2,1)S(1)} %collective-permute-done.17.near_ref, bf16[1024,640]{1,0:T(8,128)(2,1)S(1)} %collective-permute-done.16.right_ref.rest_ref, ...), custom_call_target="tpu_custom_call" | custom-call | tf_op jit(solution)/shard_map/pallas_call | solution.py:77
  131.4 3.7 %collective-permute-done.15.right_ref = bf16[1024,512]{1,0:T(8,128)(2,1)S(1)} collective-permute-done((bf16[1024,512]{1,0:T(8,128)(2,1)S(1)}, bf16[1024,512]{1,0:T(8,128)(2,1)S(1)}, u32[]{:S(2)}, u32[]{:S(2)}) %collective-permute-start.15) | collective-permute-done | bytes 1048608 | tf_op jit(solution)/shard_map/ppermute | solution.py:317
  135.1 2.3 %shard_map.79 = (bf16[256,512]{1,0:T(8,128)(2,1)}, bf16[256,512]{1,0:T(8,128)(2,1)S(1)}, bf16[256,512]{1,0:T(8,128)(2,1)S(1)}, bf16[256,512]{1,0:T(8,128)(2,1)S(1)}) custom-call(s32[5]{0:T(128)S(1)} %stack.27.place_ref, bf16[1024,1024]{1,0:T(8,128)(2,1)S(1)} %get-tuple-element.44.left_ref, bf16[1024,512]{1,0:T(8,128)(2,1)S(1)} %collective-permute-done.15.right_ref), custom_call_target="tpu_custom_call" | custom-call | tf_op jit(solution)/shard_map/pallas_call | solution.py:77
  137.3 0.7 copy-done.10
  138.1 0.7 copy-done.14
  138.8 0.7 copy-done.15
  139.4 3.6 %collective-permute-start.18 = (bf16[256,512]{1,0:T(8,128)(2,1)}, bf16[256,512]{1,0:T(8,128)(2,1)}, u32[]{:S(2)}, u32[]{:S(2)}) collective-permute-start(bf16[256,512]{1,0:T(8,128)(2,1)} %get-tuple-element.56), channel_id=1, source_target_pairs={{0,0},{1,4},{2,2},{3,6},{4,1},{5,5},{6,3},{7,7},{8,8},{9,12},{10,1... | collective-permute-start | bytes 786440 | tf_op jit(solution)/shard_map/ppermute | solution.py:317
  143.0 3.6 %collective-permute-start.19 = (bf16[256,512]{1,0:T(8,128)(2,1)}, bf16[256,512]{1,0:T(8,128)(2,1)}, u32[]{:S(2)}, u32[]{:S(2)}) collective-permute-start(bf16[256,512]{1,0:T(8,128)(2,1)} %get-tuple-element.48), channel_id=1, source_target_pairs={{0,0},{1,4},{2,2},{3,6},{4,1},{5,5},{6,3},{7,7},{8,8},{9,12},{10,1... | collective-permute-start | bytes 786440 | tf_op jit(solution)/shard_map/ppermute | solution.py:317
  146.6 1.2 collective-permute-start.23
  147.8 1.6 collective-permute-start.20
  149.4 0.9 collective-permute-start.22
  150.4 1.1 bitcast_dynamic-update-slice_fusion.11
  151.7 1.2 bitcast_dynamic-update-slice_fusion.7
  152.9 10.1 %collective-permute-done.20 = bf16[256,512]{1,0:T(8,128)(2,1)S(1)} collective-permute-done((bf16[256,512]{1,0:T(8,128)(2,1)}, bf16[256,512]{1,0:T(8,128)(2,1)S(1)}, u32[]{:S(2)}, u32[]{:S(2)}) %collective-permute-start.20) | collective-permute-done | bytes 262176 | tf_op jit(solution)/shard_map/ppermute | solution.py:317
  163.0 1.2 collective-permute-start.24
  164.5 2.1 %shard_map.80 = (bf16[256,512]{1,0:T(8,128)(2,1)S(1)}, bf16[256,512]{1,0:T(8,128)(2,1)S(1)}, bf16[256,512]{1,0:T(8,128)(2,1)S(1)}, bf16[256,512]{1,0:T(8,128)(2,...) custom-call(s32[5]{0:T(128)S(1)} %stack.27.place_ref, bf16[1024,1024]{1,0:T(8,128)(2,1)S(1)} %get-tuple-element.44.left_ref, ...), custom_call_target="tpu_custom_call" | custom-call | tf_op jit(solution)/shard_map/pallas_call | solution.py:77
  166.6 0.7 collective-permute-start.31
  167.3 9.3 %collective-permute-done.24 = bf16[256,512]{1,0:T(8,128)(2,1)S(1)} collective-permute-done((bf16[256,512]{1,0:T(8,128)(2,1)S(1)}, bf16[256,512]{1,0:T(8,128)(2,1)S(1)}, u32[]{:S(2)}, u32[]{:S(2)}) %collective-permute-start.24) | collective-permute-done | bytes 262176 | tf_op jit(solution)/shard_map/ppermute | solution.py:317
  176.7 0.7 collective-permute-start.27
  177.4 3.3 %collective-permute-start.28 = (bf16[256,512]{1,0:T(8,128)(2,1)S(1)}, bf16[256,512]{1,0:T(8,128)(2,1)S(1)}, u32[]{:S(2)}, u32[]{:S(2)}) collective-permute-start(bf16[256,512]{1,0:T(8,128)(2,1)S(1)} %get-tuple-element.63), channel_id=1, source_target_pairs={{0,1},{1,5},{2,3},{3,7},{4,0},{5,4},{6,2},{7,6},{8,9},{9,13},{10,1... | collective-permute-start | bytes 786440 | tf_op jit(solution)/shard_map/ppermute | solution.py:317
  180.7 1.4 collective-permute-start.29
  182.5 8.6 %collective-permute-done.28 = bf16[256,512]{1,0:T(8,128)(2,1)S(1)} collective-permute-done((bf16[256,512]{1,0:T(8,128)(2,1)S(1)}, bf16[256,512]{1,0:T(8,128)(2,1)S(1)}, u32[]{:S(2)}, u32[]{:S(2)}) %collective-permute-start.28) | collective-permute-done | bytes 262176 | tf_op jit(solution)/shard_map/ppermute | solution.py:317
  191.1 3.5 %collective-permute-done.30 = bf16[256,512]{1,0:T(8,128)(2,1)S(1)} collective-permute-done((bf16[256,512]{1,0:T(8,128)(2,1)S(1)}, bf16[256,512]{1,0:T(8,128)(2,1)S(1)}, u32[]{:S(2)}, u32[]{:S(2)}) %collective-permute-start.30) | collective-permute-done | bytes 262176 | tf_op jit(solution)/shard_map/ppermute | solution.py:317
  194.7 1.0 copy-done.18
  (81 shorter events, 2.3 us)
Async XLA Ops:
  0.8 1.2 copy-start.2
  2.0 1.2 copy-start.3
  3.2 0.9 copy-start.6
  4.2 0.7 copy-start.7
  7.0 30.7 %collective-permute-start.9 = (bf16[256,2304]{1,0:T(8,128)(2,1)S(1)}, bf16[256,2304]{1,0:T(8,128)(2,1)}, u32[]{:S(2)}, u32[]{:S(2)}) collective-permute-start(bf16[256,2304]{1,0:T(8,128)(2,1)S(1)} %get-tuple-element.41), channel_id=1, source_target_pairs={{0,1},{1,0},{2,3},{3,2},{4,5},{5,4},{6,7},{7,6},{8,9},{9,8},{10,11... | collective-permute-start | bytes 3538952 | tf_op jit(solution)/shard_map/ppermute | solution.py:317
  7.0 8.9 %collective-permute-start = (bf16[256,2176]{1,0:T(8,128)(2,1)}, bf16[256,2176]{1,0:T(8,128)(2,1)}, u32[]{:S(2)}, u32[]{:S(2)}) collective-permute-start(bf16[256,2176]{1,0:T(8,128)(2,1)} %get-tuple-element.37), channel_id=1, source_target_pairs={{1,4},{3,6},{4,1},{6,3},{9,12},{11,14},{12,9},{14,11},{17,20},{19,... | collective-permute-start | bytes 3342344 | tf_op jit(solution)/shard_map/ppermute | solution.py:317
  8.7 26.4 %collective-permute-start.2 = (bf16[256,2176]{1,0:T(8,128)(2,1)}, bf16[256,2176]{1,0:T(8,128)(2,1)}, u32[]{:S(2)}, u32[]{:S(2)}) collective-permute-start(bf16[256,2176]{1,0:T(8,128)(2,1)} %get-tuple-element.37), channel_id=1, source_target_pairs={{0,4},{2,6},{5,1},{7,3},{8,12},{10,14},{13,9},{15,11},{16,20},{18,... | collective-permute-start | bytes 3342344 | tf_op jit(solution)/shard_map/ppermute | solution.py:317
  14.0 25.9 %collective-permute-start.4 = (bf16[256,2304]{1,0:T(8,128)(2,1)S(1)}, bf16[256,2304]{1,0:T(8,128)(2,1)}, u32[]{:S(2)}, u32[]{:S(2)}) collective-permute-start(bf16[256,2304]{1,0:T(8,128)(2,1)S(1)} %get-tuple-element.41), channel_id=1, source_target_pairs={{0,2},{1,3},{2,0},{3,1},{4,6},{5,7},{6,4},{7,5},{8,10},{9,11},{10,... | collective-permute-start | bytes 3538952 | tf_op jit(solution)/shard_map/ppermute | solution.py:317
  15.9 51.2 %collective-permute-start.1 = (bf16[256,2304]{1,0:T(8,128)(2,1)S(1)}, bf16[256,2304]{1,0:T(8,128)(2,1)S(1)}, u32[]{:S(2)}, u32[]{:S(2)}) collective-permute-start(bf16[256,2304]{1,0:T(8,128)(2,1)S(1)} %get-tuple-element.38), channel_id=1, source_target_pairs={{0,0},{1,4},{2,2},{3,6},{4,1},{5,5},{6,3},{7,7},{8,8},{9,12},{10,1... | collective-permute-start | bytes 3538952 | tf_op jit(solution)/shard_map/ppermute | solution.py:317
  35.1 17.0 %collective-permute-start.11 = (bf16[256,2176]{1,0:T(8,128)(2,1)}, bf16[256,2176]{1,0:T(8,128)(2,1)S(1)}, u32[]{:S(2)}, u32[]{:S(2)}) collective-permute-start(bf16[256,2176]{1,0:T(8,128)(2,1)} %collective-permute-done), channel_id=1, source_target_pairs={{1,8},{3,10},{9,16},{11,18},{12,5},{14,7},{17,24},{19,26},{20,13},... | collective-permute-start | bytes 3342344 | tf_op jit(solution)/shard_map/ppermute | solution.py:317
  36.4 27.7 %collective-permute-start.12 = (bf16[256,2176]{1,0:T(8,128)(2,1)}, bf16[256,2176]{1,0:T(8,128)(2,1)S(1)}, u32[]{:S(2)}, u32[]{:S(2)}) collective-permute-start(bf16[256,2176]{1,0:T(8,128)(2,1)} %collective-permute-done.2), channel_id=1, source_target_pairs={{1,8},{3,10},{9,16},{11,18},{12,5},{14,7},{17,24},{19,26},{20,13},... | collective-permute-start | bytes 3342344 | tf_op jit(solution)/shard_map/ppermute | solution.py:317
  37.7 26.4 %collective-permute-start.7 = (bf16[256,2176]{1,0:T(8,128)(2,1)}, bf16[256,2176]{1,0:T(8,128)(2,1)S(1)}, u32[]{:S(2)}, u32[]{:S(2)}) collective-permute-start(bf16[256,2176]{1,0:T(8,128)(2,1)} %collective-permute-done), channel_id=1, source_target_pairs={{1,3},{3,1},{4,6},{6,4},{9,11},{11,9},{12,14},{14,12},{17,19},{19,... | collective-permute-start | bytes 3342344 | tf_op jit(solution)/shard_map/ppermute | solution.py:317
  39.9 25.5 %collective-permute-start.5 = (bf16[256,2176]{1,0:T(8,128)(2,1)}, bf16[256,2176]{1,0:T(8,128)(2,1)S(1)}, u32[]{:S(2)}, u32[]{:S(2)}) collective-permute-start(bf16[256,2176]{1,0:T(8,128)(2,1)} %collective-permute-done.2), channel_id=1, source_target_pairs={{1,3},{3,1},{4,6},{6,4},{9,11},{11,9},{12,14},{14,12},{17,19},{19,... | collective-permute-start | bytes 3342344 | tf_op jit(solution)/shard_map/ppermute | solution.py:317
  52.2 21.3 %collective-permute-start.3 = (bf16[256,2304]{1,0:T(8,128)(2,1)S(1)}, bf16[256,2304]{1,0:T(8,128)(2,1)S(1)}, u32[]{:S(2)}, u32[]{:S(2)}) collective-permute-start(bf16[256,2304]{1,0:T(8,128)(2,1)S(1)} %get-tuple-element.40), channel_id=1, source_target_pairs={{0,4},{1,0},{2,6},{3,2},{4,5},{5,1},{6,7},{7,3},{8,12},{9,8},{10,1... | collective-permute-start | bytes 3538952 | tf_op jit(solution)/shard_map/ppermute | solution.py:317
  64.1 11.4 %collective-permute-start.10 = (bf16[256,2304]{1,0:T(8,128)(2,1)}, bf16[256,2304]{1,0:T(8,128)(2,1)S(1)}, u32[]{:S(2)}, u32[]{:S(2)}) collective-permute-start(bf16[256,2304]{1,0:T(8,128)(2,1)} %collective-permute-done.4), channel_id=1, source_target_pairs={{0,1},{1,0},{2,3},{3,2},{4,5},{5,4},{6,7},{7,6},{8,9},{9,8},{10,11... | collective-permute-start | bytes 3538952 | tf_op jit(solution)/shard_map/ppermute | solution.py:317
  64.1 16.8 %collective-permute-start.13 = (bf16[256,2176]{1,0:T(8,128)(2,1)S(1)}, bf16[256,2176]{1,0:T(8,128)(2,1)S(1)}, u32[]{:S(2)}, u32[]{:S(2)}) collective-permute-start(bf16[256,2176]{1,0:T(8,128)(2,1)S(1)} %collective-permute-done.7), channel_id=1, source_target_pairs={{1,8},{3,10},{9,16},{11,18},{12,5},{14,7},{17,24},{19,26},{20,13},... | collective-permute-start | bytes 3342344 | tf_op jit(solution)/shard_map/ppermute | solution.py:317
  65.4 27.4 %collective-permute-start.14 = (bf16[256,2176]{1,0:T(8,128)(2,1)S(1)}, bf16[256,2176]{1,0:T(8,128)(2,1)S(1)}, u32[]{:S(2)}, u32[]{:S(2)}) collective-permute-start(bf16[256,2176]{1,0:T(8,128)(2,1)S(1)} %collective-permute-done.5), channel_id=1, source_target_pairs={{1,8},{3,10},{9,16},{11,18},{12,5},{14,7},{17,24},{19,26},{20,13},... | collective-permute-start | bytes 3342344 | tf_op jit(solution)/shard_map/ppermute | solution.py:317
  67.1 32.5 %collective-permute-start.8 = (bf16[256,2304]{1,0:T(8,128)(2,1)S(1)}, bf16[256,2304]{1,0:T(8,128)(2,1)S(1)}, u32[]{:S(2)}, u32[]{:S(2)}) collective-permute-start(bf16[256,2304]{1,0:T(8,128)(2,1)S(1)} %get-tuple-element.43), channel_id=1, source_target_pairs={{0,4},{1,2},{2,6},{3,0},{4,7},{5,1},{6,5},{7,3},{8,12},{9,10},{10,... | collective-permute-start | bytes 3538952 | tf_op jit(solution)/shard_map/ppermute | solution.py:317
  73.5 26.0 %collective-permute-start.6 = (bf16[256,2304]{1,0:T(8,128)(2,1)S(1)}, bf16[256,2304]{1,0:T(8,128)(2,1)S(1)}, u32[]{:S(2)}, u32[]{:S(2)}) collective-permute-start(bf16[256,2304]{1,0:T(8,128)(2,1)S(1)} %get-tuple-element.42), channel_id=1, source_target_pairs={{0,2},{1,4},{2,0},{3,6},{4,1},{5,7},{6,3},{7,5},{8,10},{9,12},{10,... | collective-permute-start | bytes 3538952 | tf_op jit(solution)/shard_map/ppermute | solution.py:317
  75.6 23.9 %copy-start.16 = (bf16[1024,2304]{1,0:T(8,128)(2,1)}, bf16[1024,2304]{1,0:T(8,128)(2,1)S(1)}, u32[]{:S(2)}) copy-start(bf16[1024,2304]{1,0:T(8,128)(2,1)S(1)} %constant_dynamic-update-slice_fusion.near_n.near_f.near_r) | copy-start | bytes 14155780
  118.4 4.1 %collective-permute-start.16 = (bf16[1024,640]{1,0:T(8,128)(2,1)}, bf16[1024,640]{1,0:T(8,128)(2,1)S(1)}, u32[]{:S(2)}, u32[]{:S(2)}) collective-permute-start(bf16[1024,640]{1,0:T(8,128)(2,1)} %get-tuple-element.60), channel_id=1, source_target_pairs={{0,1},{1,0},{2,3},{3,2},{4,5},{5,4},{6,7},{7,6},{8,9},{9,8},{10,11... | collective-permute-start | bytes 3932168 | tf_op jit(solution)/shard_map/ppermute | solution.py:317
  118.6 9.7 %collective-permute-start.17 = (bf16[1024,512]{1,0:T(8,128)(2,1)S(1)}, bf16[1024,512]{1,0:T(8,128)(2,1)S(1)}, u32[]{:S(2)}, u32[]{:S(2)}) collective-permute-start(bf16[1024,512]{1,0:T(8,128)(2,1)S(1)} %get-tuple-element.45), channel_id=1, source_target_pairs={{0,1},{1,0},{2,3},{3,2},{4,5},{5,4},{6,7},{7,6},{8,9},{9,8},{10,11... | collective-permute-start | bytes 3145736 | tf_op jit(solution)/shard_map/ppermute | solution.py:317
  119.0 16.1 %collective-permute-start.15 = (bf16[1024,512]{1,0:T(8,128)(2,1)S(1)}, bf16[1024,512]{1,0:T(8,128)(2,1)S(1)}, u32[]{:S(2)}, u32[]{:S(2)}) collective-permute-start(bf16[1024,512]{1,0:T(8,128)(2,1)S(1)} %get-tuple-element.45), channel_id=1, source_target_pairs={{1,8},{3,10},{5,12},{7,14},{8,1},{9,16},{10,3},{11,18},{12,5},{13,... | collective-permute-start | bytes 3145736 | tf_op jit(solution)/shard_map/ppermute | solution.py:317
  122.5 42.0 %collective-permute-start.26 = (bf16[1024,640]{1,0:T(8,128)(2,1)}, bf16[1024,640]{1,0:T(8,128)(2,1)S(1)}, u32[]{:S(2)}, u32[]{:S(2)}) collective-permute-start(bf16[1024,640]{1,0:T(8,128)(2,1)} %get-tuple-element.60), channel_id=1, source_target_pairs={{1,8},{3,10},{5,12},{7,14},{8,1},{9,16},{10,3},{11,18},{12,5},{13,... | collective-permute-start | bytes 3932168 | tf_op jit(solution)/shard_map/ppermute | solution.py:317
  126.8 0.7 copy-start.12
  127.5 0.7 copy-start.13
  128.2 3.1 %copy-start.8 = (bf16[256,512]{1,0:T(8,128)(2,1)}, bf16[256,512]{1,0:T(8,128)(2,1)S(1)}, u32[]{:S(2)}) copy-start(bf16[256,512]{1,0:T(8,128)(2,1)S(1)} %get-tuple-element.51) | copy-start | bytes 786436
  131.4 6.0 %copy-start = (f32[1024,512]{1,0:T(8,128)}, f32[1024,512]{1,0:T(8,128)S(1)}, u32[]{:S(2)}) copy-start(f32[1024,512]{1,0:T(8,128)S(1)} %get-tuple-element.54.excess_ref) | copy-start | bytes 6291460
  131.4 6.0 %copy-start.4 = (f32[1024,128]{1,0:T(8,128)}, f32[1024,128]{1,0:T(8,128)S(1)}, u32[]{:S(2)}) copy-start(f32[1024,128]{1,0:T(8,128)S(1)} %get-tuple-element.61.rhs_ref) | copy-start | bytes 1572868
  137.3 0.7 copy-start.10
  138.1 0.7 copy-start.14
  138.8 0.7 copy-start.15
  139.4 8.4 %collective-permute-start.18 = (bf16[256,512]{1,0:T(8,128)(2,1)}, bf16[256,512]{1,0:T(8,128)(2,1)}, u32[]{:S(2)}, u32[]{:S(2)}) collective-permute-start(bf16[256,512]{1,0:T(8,128)(2,1)} %get-tuple-element.56), channel_id=1, source_target_pairs={{0,0},{1,4},{2,2},{3,6},{4,1},{5,5},{6,3},{7,7},{8,8},{9,12},{10,1... | collective-permute-start | bytes 786440 | tf_op jit(solution)/shard_map/ppermute | solution.py:317
  143.0 6.4 %collective-permute-start.19 = (bf16[256,512]{1,0:T(8,128)(2,1)}, bf16[256,512]{1,0:T(8,128)(2,1)}, u32[]{:S(2)}, u32[]{:S(2)}) collective-permute-start(bf16[256,512]{1,0:T(8,128)(2,1)} %get-tuple-element.48), channel_id=1, source_target_pairs={{0,0},{1,4},{2,2},{3,6},{4,1},{5,5},{6,3},{7,7},{8,8},{9,12},{10,1... | collective-permute-start | bytes 786440 | tf_op jit(solution)/shard_map/ppermute | solution.py:317
  146.6 16.4 %collective-permute-start.21 = (bf16[256,512]{1,0:T(8,128)(2,1)}, bf16[256,512]{1,0:T(8,128)(2,1)S(1)}, u32[]{:S(2)}, u32[]{:S(2)}) collective-permute-start(bf16[256,512]{1,0:T(8,128)(2,1)} %copy-done.13), channel_id=1, source_target_pairs={{0,1},{1,5},{2,3},{3,7},{4,0},{5,4},{6,2},{7,6},{8,9},{9,13},{10,1... | collective-permute-start | bytes 786440 | tf_op jit(solution)/shard_map/ppermute | solution.py:317
  146.6 17.7 %collective-permute-start.23 = (bf16[256,512]{1,0:T(8,128)(2,1)}, bf16[256,512]{1,0:T(8,128)(2,1)S(1)}, u32[]{:S(2)}, u32[]{:S(2)}) collective-permute-start(bf16[256,512]{1,0:T(8,128)(2,1)} %copy-done.12), channel_id=1, source_target_pairs={{0,2},{1,6},{2,0},{3,4},{4,3},{5,7},{6,1},{7,5},{8,10},{9,14},{10,... | collective-permute-start | bytes 786440 | tf_op jit(solution)/shard_map/ppermute | solution.py:317
  147.8 15.2 %collective-permute-start.20 = (bf16[256,512]{1,0:T(8,128)(2,1)}, bf16[256,512]{1,0:T(8,128)(2,1)S(1)}, u32[]{:S(2)}, u32[]{:S(2)}) collective-permute-start(bf16[256,512]{1,0:T(8,128)(2,1)} %copy-done.15), channel_id=1, source_target_pairs={{0,1},{1,5},{2,3},{3,7},{4,0},{5,4},{6,2},{7,6},{8,9},{9,13},{10,1... | collective-permute-start | bytes 786440 | tf_op jit(solution)/shard_map/ppermute | solution.py:317
  149.4 14.9 %collective-permute-start.22 = (bf16[256,512]{1,0:T(8,128)(2,1)}, bf16[256,512]{1,0:T(8,128)(2,1)S(1)}, u32[]{:S(2)}, u32[]{:S(2)}) collective-permute-start(bf16[256,512]{1,0:T(8,128)(2,1)} %copy-done.14), channel_id=1, source_target_pairs={{0,2},{1,6},{2,0},{3,4},{4,3},{5,7},{6,1},{7,5},{8,10},{9,14},{10,... | collective-permute-start | bytes 786440 | tf_op jit(solution)/shard_map/ppermute | solution.py:317
  150.4 12.6 %copy-start.9 = (bf16[256,512]{1,0:T(8,128)(2,1)S(1)}, bf16[256,512]{1,0:T(8,128)(2,1)}, u32[]{:S(2)}) copy-start(bf16[256,512]{1,0:T(8,128)(2,1)} %copy-done.8) | copy-start | bytes 786436
  150.4 12.6 %copy-start.11 = (bf16[256,512]{1,0:T(8,128)(2,1)S(1)}, bf16[256,512]{1,0:T(8,128)(2,1)}, u32[]{:S(2)}) copy-start(bf16[256,512]{1,0:T(8,128)(2,1)} %copy-done.10) | copy-start | bytes 786436
  151.7 12.8 %copy-start.1 = (f32[1024,512]{1,0:T(8,128)S(1)}, f32[1024,512]{1,0:T(8,128)}, u32[]{:S(2)}) copy-start(f32[1024,512]{1,0:T(8,128)} %copy-done) | copy-start | bytes 6291460
  151.7 12.8 %copy-start.5 = (f32[1024,128]{1,0:T(8,128)S(1)}, f32[1024,128]{1,0:T(8,128)}, u32[]{:S(2)}) copy-start(f32[1024,128]{1,0:T(8,128)} %copy-done.4) | copy-start | bytes 1572868
  163.0 13.5 %collective-permute-start.25 = (bf16[256,512]{1,0:T(8,128)(2,1)S(1)}, bf16[256,512]{1,0:T(8,128)(2,1)S(1)}, u32[]{:S(2)}, u32[]{:S(2)}) collective-permute-start(bf16[256,512]{1,0:T(8,128)(2,1)S(1)} %copy-done.9), channel_id=1, source_target_pairs={{0,3},{1,7},{2,1},{3,5},{4,2},{5,6},{6,0},{7,4},{8,11},{9,15},{10,... | collective-permute-start | bytes 786440 | tf_op jit(solution)/shard_map/ppermute | solution.py:317
  163.0 13.5 %collective-permute-start.24 = (bf16[256,512]{1,0:T(8,128)(2,1)S(1)}, bf16[256,512]{1,0:T(8,128)(2,1)S(1)}, u32[]{:S(2)}, u32[]{:S(2)}) collective-permute-start(bf16[256,512]{1,0:T(8,128)(2,1)S(1)} %copy-done.11), channel_id=1, source_target_pairs={{0,3},{1,7},{2,1},{3,5},{4,2},{5,6},{6,0},{7,4},{8,11},{9,15},{10,... | collective-permute-start | bytes 786440 | tf_op jit(solution)/shard_map/ppermute | solution.py:317
  166.6 15.6 %collective-permute-start.31 = (f32[256,128]{1,0:T(8,128)S(1)}, f32[256,128]{1,0:T(8,128)S(1)}, u32[]{:S(2)}, u32[]{:S(2)}) collective-permute-start(f32[256,128]{1,0:T(8,128)S(1)} %get-tuple-element.66), channel_id=1, source_target_pairs={{0,0},{1,4},{2,2},{3,6},{4,1},{5,5},{6,3},{7,7},{8,8},{9,12},{10,1... | collective-permute-start | bytes 393224 | tf_op jit(solution)/shard_map/ppermute | solution.py:317
  176.6 14.4 %copy-start.17 = (bf16[2,256,1024]{2,1,0:T(8,128)(2,1)}, bf16[2,256,1024]{2,1,0:T(8,128)(2,1)S(1)}, u32[]{:S(2)}) copy-start(bf16[2,256,1024]{2,1,0:T(8,128)(2,1)S(1)} %get-tuple-element.71) | copy-start | bytes 3145732
  176.7 14.4 %copy-start.19 = (bf16[2,256,1024]{2,1,0:T(8,128)(2,1)}, bf16[2,256,1024]{2,1,0:T(8,128)(2,1)S(1)}, u32[]{:S(2)}) copy-start(bf16[2,256,1024]{2,1,0:T(8,128)(2,1)S(1)} %get-tuple-element.72) | copy-start | bytes 3145732
  176.7 5.6 %collective-permute-start.32 = (f32[256,128]{1,0:T(8,128)S(1)}, f32[256,128]{1,0:T(8,128)S(1)}, u32[]{:S(2)}, u32[]{:S(2)}) collective-permute-start(f32[256,128]{1,0:T(8,128)S(1)} %get-tuple-element.67), channel_id=1, source_target_pairs={{0,1},{1,5},{2,3},{3,7},{4,0},{5,4},{6,2},{7,6},{8,9},{9,13},{10,1... | collective-permute-start | bytes 393224 | tf_op jit(solution)/shard_map/ppermute | solution.py:317
  176.7 5.5 %collective-permute-start.27 = (bf16[256,512]{1,0:T(8,128)(2,1)S(1)}, bf16[256,512]{1,0:T(8,128)(2,1)S(1)}, u32[]{:S(2)}, u32[]{:S(2)}) collective-permute-start(bf16[256,512]{1,0:T(8,128)(2,1)S(1)} %get-tuple-element.62), channel_id=1, source_target_pairs={{0,0},{1,4},{2,2},{3,6},{4,1},{5,5},{6,3},{7,7},{8,8},{9,12},{10,1... | collective-permute-start | bytes 786440 | tf_op jit(solution)/shard_map/ppermute | solution.py:317
  177.4 13.6 %collective-permute-start.28 = (bf16[256,512]{1,0:T(8,128)(2,1)S(1)}, bf16[256,512]{1,0:T(8,128)(2,1)S(1)}, u32[]{:S(2)}, u32[]{:S(2)}) collective-permute-start(bf16[256,512]{1,0:T(8,128)(2,1)S(1)} %get-tuple-element.63), channel_id=1, source_target_pairs={{0,1},{1,5},{2,3},{3,7},{4,0},{5,4},{6,2},{7,6},{8,9},{9,13},{10,1... | collective-permute-start | bytes 786440 | tf_op jit(solution)/shard_map/ppermute | solution.py:317
  180.7 10.3 %collective-permute-start.29 = (bf16[256,512]{1,0:T(8,128)(2,1)S(1)}, bf16[256,512]{1,0:T(8,128)(2,1)S(1)}, u32[]{:S(2)}, u32[]{:S(2)}) collective-permute-start(bf16[256,512]{1,0:T(8,128)(2,1)S(1)} %get-tuple-element.64), channel_id=1, source_target_pairs={{0,2},{1,6},{2,0},{3,4},{4,3},{5,7},{6,1},{7,5},{8,10},{9,14},{10,... | collective-permute-start | bytes 786440 | tf_op jit(solution)/shard_map/ppermute | solution.py:317
  182.2 12.5 %collective-permute-start.30 = (bf16[256,512]{1,0:T(8,128)(2,1)S(1)}, bf16[256,512]{1,0:T(8,128)(2,1)S(1)}, u32[]{:S(2)}, u32[]{:S(2)}) collective-permute-start(bf16[256,512]{1,0:T(8,128)(2,1)S(1)} %get-tuple-element.65), channel_id=1, source_target_pairs={{0,3},{1,7},{2,1},{3,5},{4,2},{5,6},{6,0},{7,4},{8,11},{9,15},{10,... | collective-permute-start | bytes 786440 | tf_op jit(solution)/shard_map/ppermute | solution.py:317
  182.3 8.9 %copy-start.20 = (f32[2,256,128]{2,1,0:T(8,128)}, f32[2,256,128]{2,1,0:T(8,128)S(1)}, u32[]{:S(2)}) copy-start(f32[2,256,128]{2,1,0:T(8,128)S(1)} %bitcast_dynamic-update-slice_fusion.12) | copy-start | bytes 786436
  194.7 1.0 copy-start.18
